TPU v7x, 256 devices: a whole 4x4x8 slice. The times are simulated.
256 devices in a mesh: dp: 64 (over z, y, core), expert: 4 (over x).
Axes of the slice: x: 4, y: 4, z: 8, core: 2. Of those that a mesh axis runs over, the one named last changes fastest.
Arguments:
- tokens: bfloat16 [32768, 2048], P(('dp', 'expert')), may hold values from -6 to 6
- cotangent: bfloat16 [32768, 2048], P(('dp', 'expert')), may hold values from -6 to 6
- expert_ids: int32 [32768, 2], P(('dp', 'expert')), may hold values from 0 to 3, all different within a row; in each aligned block of 128 rows (0 to 127, 128 to 255, ...) at most 80 rows name the same one
- gate_probs: float32 [32768, 2], P(('dp', 'expert')), may hold values from 0.2 to 1
- gate_up_weight: bfloat16 [4, 2048, 1024], P('expert'), may hold values from -0.125 to 0.125
- down_weight: bfloat16 [4, 512, 2048], P('expert'), may hold values from -0.25 to 0.25
- down_residual: bfloat16 [64, 4, 512, 2048], P('dp', 'expert'), may hold values from -32 to 32
Outputs:
- token_grad: bfloat16 [32768, 2048], P(('dp', 'expert'))
- grad_gate_up: float32 [4, 2048, 1024], P('expert', 'dp')
- grad_down: float32 [4, 512, 2048], P('expert', 'dp')
Inputs may be any that keep to these rules, and one draw needn't show every extreme that they name: `expert_ids`: each token names 2 different experts. Among the tokens of one device no expert is named by more than 80 tokens, and in some device's tokens one expert is named by exactly 80.
All inputs are finite; a program needn't handle non-finite values.
Results may differ from a plain program's by a relative error of at most 0.0065.
Values may be sent and summed in bfloat16 or wider, within the bound.
A program may use at most 128 MiB of HBM per device.

v0:
```python
import jax
import jax.numpy as jnp
from jax import lax
from jax.sharding import PartitionSpec as P


def expert_forward(token_rows, gate_up):
    hidden_units = gate_up.shape[1] // 2
    projected = jnp.dot(token_rows, gate_up, preferred_element_type=jnp.float32)
    gate_part = projected[:, :hidden_units]
    up_part = projected[:, hidden_units:]
    gate_sig = jax.nn.sigmoid(gate_part)
    activated = gate_part * gate_sig
    hidden = (activated * up_part).astype(jnp.bfloat16)
    return (gate_part, up_part, gate_sig, activated, hidden)


def expert_backward(token_rows, scaled, forward, gate_up, down_matrix):
    gate_part, up_part, gate_sig, activated, hidden = forward
    back_hidden = jnp.dot(scaled, down_matrix.T, preferred_element_type=jnp.float32)
    back_gate = back_hidden * up_part * gate_sig * (1.0 + gate_part * (1.0 - gate_sig))
    back_up = back_hidden * activated
    back_both = jnp.concatenate([back_gate, back_up], axis=1).astype(jnp.bfloat16)
    token_part = jnp.dot(back_both, gate_up.T, preferred_element_type=jnp.float32).astype(
        jnp.bfloat16
    )
    contract = (((0,), (0,)), ((), ()))
    gate_up_term = lax.dot_general(
        token_rows, back_both, contract, preferred_element_type=jnp.float32
    )
    down_term = lax.dot_general(hidden, scaled, contract, preferred_element_type=jnp.float32)
    return (token_part, gate_up_term, down_term)


def on_device(
    tokens, cotangent, expert_ids, gate_probs, gate_up_weight, down_weight, down_residual
):
    tok_rows, model_width = tokens.shape
    expert_count = lax.axis_size("expert")
    capacity = tok_rows * 5 // 8
    expert_range = jnp.arange(expert_count, dtype=jnp.int32)
    route_hit = expert_ids[:, :, None] == expert_range[None, None, :]
    member = jnp.any(route_hit, axis=1).astype(jnp.int32)
    route_weight = jnp.sum(jnp.where(route_hit, gate_probs[:, :, None], 0.0), axis=1)
    slot_index = jnp.cumsum(member, axis=0) - member
    slot_range = jnp.arange(capacity, dtype=jnp.int32)
    placed = (member.T[:, None, :] == 1) & (slot_index.T[:, None, :] == slot_range[None, :, None])
    token_range = jnp.arange(tok_rows, dtype=jnp.int32)
    filled = jnp.any(placed, axis=2)
    source_row = jnp.where(
        filled, jnp.sum(jnp.where(placed, token_range[None, None, :], 0), axis=2), tok_rows
    )
    slot_weight = jnp.sum(jnp.where(placed, route_weight.T[:, None, :], 0.0), axis=2)
    zero_row = jnp.zeros((1, model_width), jnp.bfloat16)
    send_rows = jnp.concatenate([tokens, zero_row], axis=0)[source_row]
    send_grads = (
        jnp.concatenate([cotangent, zero_row], axis=0)[source_row].astype(jnp.float32)
        * slot_weight[:, :, None]
    ).astype(jnp.bfloat16)
    gate_up = gate_up_weight[0]
    down_matrix = down_weight[0]
    total_rows = expert_count * capacity
    got_rows, got_grads = (
        lax.all_to_all(send_rows, "expert", split_axis=0, concat_axis=0, tiled=True),
        lax.all_to_all(send_grads, "expert", split_axis=0, concat_axis=0, tiled=True),
    )
    flat_rows = got_rows.reshape(total_rows, model_width)
    forward = expert_forward(flat_rows, gate_up)
    flat_grads = got_grads.reshape(total_rows, model_width)
    token_part, gate_up_term, down_term = expert_backward(
        flat_rows, flat_grads, forward, gate_up, down_matrix
    )
    returned = lax.all_to_all(
        token_part.reshape(expert_count, capacity, model_width),
        "expert",
        split_axis=0,
        concat_axis=0,
        tiled=True,
    )
    returned = returned.reshape(total_rows, model_width)
    pick_rows = expert_ids * capacity + jnp.take_along_axis(slot_index, expert_ids, axis=1)
    token_grad = jnp.sum(returned[pick_rows].astype(jnp.float32), axis=1).astype(jnp.bfloat16)
    gate_up_round = gate_up_term.astype(jnp.bfloat16)
    down_round = (down_term + down_residual[0, 0].astype(jnp.float32)).astype(jnp.bfloat16)
    group_count = lax.axis_size("dp")
    gate_up_wide = lax.optimization_barrier(gate_up_round).astype(jnp.float32)
    down_wide = lax.optimization_barrier(down_round).astype(jnp.float32)
    gate_up_part, down_part = (
        lax.psum_scatter(gate_up_wide, "dp", scatter_dimension=0, tiled=True),
        lax.psum_scatter(down_wide, "dp", scatter_dimension=0, tiled=True),
    )
    factor = 1.0 / group_count
    return (token_grad, (gate_up_part * factor)[None], (down_part * factor)[None])


def solution(mesh):
    placed = (
        P(("dp", "expert"), None),
        P(("dp", "expert"), None),
        P(("dp", "expert"), None),
        P(("dp", "expert"), None),
        P("expert", None, None),
        P("expert", None, None),
        P("dp", "expert", None, None),
    )
    return jax.shard_map(
        on_device,
        mesh=mesh,
        in_specs=placed,
        out_specs=(P(("dp", "expert"), None), P("expert", "dp", None), P("expert", "dp", None)),
        check_vma=False,
    )
```

profile of v0, /device:TPU:1, one launch (start us, length us, event | category | flops | bytes accessed | tf_op | source)
XLA Modules:
  0.0 398.2 jit_solution(4403838437266869531)
XLA Ops:
  7.2 0.8 fusion.16
  8.1 0.2 reduce_window_sum.11
  8.4 0.2 fusion.13
  8.6 0.2 select_reduce_fusion.1
  8.8 1.1 concatenate.11
  9.9 3.0 gather_fusion.1
  12.9 5.0 %all-to-all-start.1 = ((bf16[4,80,2048]{2,1,0:T(8,128)(2,1)}), bf16[4,80,2048]{2,1,0:T(8,128)(2,1)}, u32[]{:S(2)}, u32[]{:S(2)}) async-start(bf16[4,80,2048]{2,1,0:T(8,128)(2,1)} %bitcast.47), calls=%async_computation.1 | async-start | bytes 2621440 | tf_op jit(solution)/shard_map/all_to_all | solution.py:64
  18.0 3.0 gather_fusion
  21.0 0.1 select_reduce_fusion
  21.2 2.7 fusion.8
  23.9 9.5 %all-to-all-done.1 = bf16[4,80,2048]{2,1,0:T(8,128)(2,1)} async-done(((bf16[4,80,2048]{2,1,0:T(8,128)(2,1)}), bf16[4,80,2048]{2,1,0:T(8,128)(2,1)}, u32[]{:S(2)}, u32[]{:S(2)}) %all-to-all-start.1) | async-done | bytes 1310752 | tf_op jit(solution)/shard_map/all_to_all | solution.py:64
  33.4 3.5 all-to-all-start
  37.0 5.3 %fusion.3 = f32[320,1024]{1,0:T(8,128)} fusion(bf16[320,2048]{1,0:T(8,128)(2,1)} %bitcast.8, bf16[1,2048,1024]{2,1,0:T(8,128)(2,1)} %param.11), kind=kOutput, calls=%fused_computation.8 | convolution fusion | flops 1342177280 | bytes 6815744 | tf_op jit(solution)/shard_map/dot_general | solution.py:9
  42.2 8.8 %all-to-all-done = bf16[4,80,2048]{2,1,0:T(8,128)(2,1)S(1)} async-done(((bf16[4,80,2048]{2,1,0:T(8,128)(2,1)}), bf16[4,80,2048]{2,1,0:T(8,128)(2,1)S(1)}, u32[]{:S(2)}, u32[]{:S(2)}) %all-to-all-start) | async-done | bytes 1310752 | tf_op jit(solution)/shard_map/all_to_all | solution.py:65
  51.0 2.3 multiply_convert_fusion.2
  53.3 0.7 copy-done.6
  54.1 3.7 convolution_convert_fusion
  57.8 4.3 %convert_element_type.44 = f32[2048,1024]{1,0:T(8,128)} convert(bf16[2048,1024]{1,0:T(8,128)(2,1)S(1)} %convolution_convert_fusion) | non-fusion elementwise | flops 2097152 | bytes 12582912 | tf_op jit(solution)/shard_map/convert_element_type | solution.py:86
  62.3 0.1 reshape.88
  62.4 2.4 gather_fusion.3
  64.8 0.1 reshape.91
  65.1 0.1 reshape.82
  65.3 0.6 dynamic-slice
  66.6 4.9 %fusion = bf16[512,2048]{1,0:T(8,128)(2,1)} fusion(bf16[320,2048]{1,0:T(8,128)(2,1)S(1)} %bitcast.50, bf16[1,1,512,2048]{3,2,1,0:T(8,128)(2,1)} %param.13, f32[320,1024]{1,0:T(8,128)} %fusion.3), kind=kOutput, calls=%fused_computation.5 | convolution fusion | flops 675217408 | bytes 6815744 | tf_op jit(solution)/shard_map/dot_general | solution.py:31
  71.5 2.6 fusion.5
  74.1 3.5 all-to-all-start.2
  77.6 302.8 %all-reduce.4 = f32[512,2048]{1,0:T(8,128)} all-reduce(bf16[512,2048]{1,0:T(8,128)(2,1)} %fusion), channel_id=3, replica_groups=mesh['dp'=64,'expert'=4] {'dp'}, use_global_device_ids=true, to_apply=%region_8.9.clone | all-reduce | flops 1048576 | bytes 6291456
  380.5 1.5 fusion.15
  382.0 2.4 gather_fusion.2
  384.4 1.7 reshape.85
  386.1 3.6 reduce_sum.42
  389.8 1.6 multiply_bitcast_fusion
  (38 shorter events, 0.9 us)
Async XLA Ops:
  7.2 43.8 %copy-start = (bf16[1,512,2048]{2,1,0:T(8,128)(2,1)S(1)}, bf16[1,512,2048]{2,1,0:T(8,128)(2,1)}, u32[]{:S(2)}) copy-start(bf16[1,512,2048]{2,1,0:T(8,128)(2,1)} %param.12) | copy-start | bytes 6291460
  12.9 5.0 %copy-start.1 = (bf16[128,2048]{1,0:T(8,128)(2,1)S(1)}, bf16[128,2048]{1,0:T(8,128)(2,1)}, u32[]{:S(2)}) copy-start(bf16[128,2048]{1,0:T(8,128)(2,1)} %param.8) | copy-start | bytes 1572868
  12.9 20.4 %all-to-all-start.1 = ((bf16[4,80,2048]{2,1,0:T(8,128)(2,1)}), bf16[4,80,2048]{2,1,0:T(8,128)(2,1)}, u32[]{:S(2)}, u32[]{:S(2)}) async-start(bf16[4,80,2048]{2,1,0:T(8,128)(2,1)} %bitcast.47), calls=%async_computation.1 | async-start | bytes 2621440 | tf_op jit(solution)/shard_map/all_to_all | solution.py:64
  18.0 3.1 copy-start.2
  18.0 3.1 copy-start.3
  33.4 17.6 %all-to-all-start = ((bf16[4,80,2048]{2,1,0:T(8,128)(2,1)}), bf16[4,80,2048]{2,1,0:T(8,128)(2,1)S(1)}, u32[]{:S(2)}, u32[]{:S(2)}) async-start(bf16[4,80,2048]{2,1,0:T(8,128)(2,1)} %fusion.8), calls=%async_computation | async-start | bytes 2621440 | tf_op jit(solution)/shard_map/all_to_all | solution.py:65
  36.9 352.9 %reduce-scatter.2.cloned.1.call-start = ((), (), s32[]{:S(2)}) async-start(), calls=%async_computation.4 | async-start | bytes 8519680 | tf_op jit(solution)/shard_map/reduce_scatter | solution.py:89
  53.3 0.7 copy-start.6
  53.3 0.8 copy-start.8
  62.4 2.9 copy-start.5
  66.6 4.9 %copy-start.4 = (bf16[1,2048,1024]{2,1,0:T(8,128)(2,1)S(1)}, bf16[1,2048,1024]{2,1,0:T(8,128)(2,1)}, u32[]{:S(2)}) copy-start(bf16[1,2048,1024]{2,1,0:T(8,128)(2,1)} %param.11) | copy-start | bytes 12582916
  66.6 4.9 %copy-start.7 = (bf16[320,512]{1,0:T(8,128)(2,1)S(1)}, bf16[320,512]{1,0:T(8,128)(2,1)}, u32[]{:S(2)}) copy-start(bf16[320,512]{1,0:T(8,128)(2,1)} %copy-done.6) | copy-start | bytes 983044
  66.6 4.9 %copy-start.9 = (bf16[320,512]{1,0:T(8,128)(2,1)S(1)}, bf16[320,512]{1,0:T(8,128)(2,1)}, u32[]{:S(2)}) copy-start(bf16[320,512]{1,0:T(8,128)(2,1)} %copy-done.8) | copy-start | bytes 983044
  74.1 307.9 %all-to-all-start.2 = ((bf16[4,80,2048]{2,1,0:T(8,128)(2,1)}), bf16[4,80,2048]{2,1,0:T(8,128)(2,1)S(1)}, u32[]{:S(2)}, u32[]{:S(2)}) async-start(bf16[4,80,2048]{2,1,0:T(8,128)(2,1)} %bitcast.51), calls=%async_computation.2 | async-start | bytes 2621440 | tf_op jit(solution)/shard_map/all_to_all | solution.py:73
Sparse Core Ops, SparseCore 0:
  62.2 156.1 reduce-scatter.1
where the time goes:
time: 403 us; the launch traced here: 398 us
  blocking collectives  303 us (75%)
  matrix products  18.8 us (5%)
  waiting for transfers between devices  18.3 us (5%)
  local copies, waits for them, and re-layouts  16.2 us (4%)
  other arithmetic  15.2 us (4%)
  between operations  14.9 us (4%)
  starting transfers between devices  12.1 us (3%)
    unnamed x1, blocking collectives  303 us
    all_to_all x1, waiting for transfers between devices, on_device(): lax.all_to_all(send_rows, 'expert', split_axis=0, concat_axis=0, tiled=True)  9.48 us
    all_to_all x1, waiting for transfers between devices, on_device(): lax.all_to_all(send_grads, 'expert', split_axis=0, concat_axis=0, tiled=T...  8.76 us
  transfers between devices with their start and end apart: 4, of which 2 were waited for; matrix products, arithmetic and copies ran while one was open for 8% of the time, Pallas kernels for 0%

commit v1 on v0

--- a/solution.py
+++ b/solution.py
@@ -1,7 +1,328 @@
 import jax
 import jax.numpy as jnp
 from jax import lax
+from jax.experimental import pallas as pl
+from jax.experimental.pallas import tpu as pltpu
 from jax.sharding import PartitionSpec as P
+
+MESH = pl.DeviceIdType.MESH
+CHIPS_Z, CHIPS_Y, CORES = 8, 4, 2
+SHARE = 48
+GATE_ROWS, DOWN_ROWS = 32, 8
+WIDTH = 1024
+COLS_A = 512
+COLS_B = WIDTH - COLS_A
+ORDER_Z = (4, 3, -3, 2, -2, 1, -1, 0)
+ORDER_Y = (2, 1, -1, 0)
+
+
+def scatter_kernel(
+    gate_ref, down_ref, gate_out, down_out,
+    give_a, give_b, got_a, got_b, own_a, own_b,
+    az_buf, ay_buf, by_buf, bz_buf,
+    pair_a_sem, pair_b_sem, az_sem, ay_sem, by_sem, bz_sem,
+):
+    me, col = lax.axis_index("dp"), lax.axis_index("expert")
+    z, y, core = me // (CHIPS_Y * CORES), (me // CORES) % CHIPS_Y, me % CORES
+
+    def at(zz, yy, cc):
+        return (((zz + CHIPS_Z) % CHIPS_Z) * CHIPS_Y + (yy + CHIPS_Y) % CHIPS_Y) * CORES + cc
+
+    def zi(off):
+        return (z + off + CHIPS_Z) % CHIPS_Z
+
+    def yi(off):
+        return (y + off + CHIPS_Y) % CHIPS_Y
+
+    partner = at(z, y, 1 - core)
+    z_next, z_prev = at(z + 1, y, core), at(z - 1, y, core)
+    y_next, y_prev = at(z, y + 1, core), at(z, y - 1, core)
+    barrier = pltpu.get_barrier_semaphore()
+    for device in (partner, z_next, z_prev, y_next, y_prev):
+        pl.semaphore_signal(barrier, inc=1, device_id=(device, col), device_id_type=MESH)
+    pl.semaphore_wait(barrier, 5)
+
+    started = []
+
+    def send(src, dst, sems, index, device):
+        copy = pltpu.make_async_remote_copy(
+            src_ref=src, dst_ref=dst, send_sem=sems.at[(0, *index)], recv_sem=sems.at[(1, *index)],
+            device_id=(device, col), device_id_type=MESH,
+        )
+        copy.start()
+        started.append(copy)
+        return copy
+
+    def term(zz, yy, cc, lo, hi):
+        share = (zz * CHIPS_Y + yy) * CORES + cc
+        gate_rows = pl.ds(pl.multiple_of(share * GATE_ROWS, GATE_ROWS), GATE_ROWS)
+        down_rows = pl.ds(pl.multiple_of(share * DOWN_ROWS, DOWN_ROWS), DOWN_ROWS)
+        low = jnp.concatenate(
+            [down_ref[down_rows, lo:hi], down_ref[down_rows, WIDTH + lo : WIDTH + hi]], axis=0
+        )
+        return gate_ref[gate_rows, lo:hi], low
+
+    def put(ref, index, values):
+        gate_part, down_part = values
+        ref[(*index, slice(0, 32))] = gate_part.astype(jnp.bfloat16)
+        ref[(*index, slice(32, 48))] = down_part.astype(jnp.bfloat16)
+
+    pair_copies = {}
+
+    def give_group_a(off):
+        def body(yy, carry):
+            put(give_a, (zi(off), yy), term(zi(off), yy, 1 - core, 0, COLS_A))
+            return carry
+        lax.fori_loop(0, CHIPS_Y, body, 0)
+        pair_copies["a", off] = send(
+            give_a.at[zi(off)], got_a.at[zi(off)], pair_a_sem, (ORDER_Z.index(off),), partner
+        )
+
+    def give_group_b(off):
+        def body(zz, carry):
+            put(give_b, (yi(off), zz), term(zz, yi(off), 1 - core, COLS_A, WIDTH))
+            return carry
+        lax.fori_loop(0, CHIPS_Z, body, 0)
+        pair_copies["b", off] = send(
+            give_b.at[yi(off)], got_b.at[yi(off)], pair_b_sem, (ORDER_Y.index(off),), partner
+        )
+
+    def wide(value):
+        return value.astype(jnp.float32)
+
+    def take_group_a(off):
+        pair_copies["a", off].wait_recv()
+        def body(yy, carry):
+            gate_part, down_part = term(zi(off), yy, core, 0, COLS_A)
+            got = wide(got_a[zi(off), yy])
+            put(own_a, (zi(off), yy), (gate_part + got[:32], down_part + got[32:]))
+            return carry
+        lax.fori_loop(0, CHIPS_Y, body, 0)
+
+    def take_group_b(off):
+        pair_copies["b", off].wait_recv()
+        def body(zz, carry):
+            gate_part, down_part = term(zz, yi(off), core, COLS_A, WIDTH)
+            got = wide(got_b[yi(off), zz])
+            put(own_b, (yi(off), zz), (gate_part + got[:32], down_part + got[32:]))
+            return carry
+        lax.fori_loop(0, CHIPS_Z, body, 0)
+
+    def add_into(ref, index, part):
+        ref[index] = (wide(ref[index]) + wide(part)).astype(jnp.bfloat16)
+
+    copies = {}
+
+    def a_z(side, step, yy, received):
+        off = (5 - step) if side == 0 else step - 5
+        if received:
+            copies["az", side, step - 1, yy].wait_recv()
+            add_into(own_a, (zi(off), yy), az_buf[side, step - 2, yy])
+        copies["az", side, step, yy] = send(
+            own_a.at[zi(off), yy], az_buf.at[side, step - 1, yy], az_sem, (side, step - 1, yy),
+            z_next if side == 0 else z_prev,
+        )
+
+    def a_z_end(yy):
+        total = wide(own_a[z, yy])
+        for side in range(2):
+            copies["az", side, 4, yy].wait_recv()
+            total = total + wide(az_buf[side, 3, yy])
+        own_a[z, yy] = total.astype(jnp.bfloat16)
+
+    half_rows = {("ay", 0): slice(0, 32), ("ay", 1): slice(32, 48), ("bz", 0): slice(32, 48), ("bz", 1): slice(0, 32)}
+
+    def a_y(side, step):
+        off = (3 - step) if side == 0 else step - 3
+        rows = half_rows["ay", side]
+        if step == 1:
+            copies["ay", side, 1] = send(
+                own_a.at[z, yi(off), rows], ay_buf.at[side, 0, rows], ay_sem, (side, 0),
+                y_next if side == 0 else y_prev,
+            )
+            return
+        copies["ay", side, 1].wait_recv()
+        add_into(own_a, (z, yi(off), rows), ay_buf[side, 0, rows])
+        copies["ay", side, 2] = send(
+            own_a.at[z, yi(off)], ay_buf.at[side, 1], ay_sem, (side, 1),
+            y_next if side == 0 else y_prev,
+        )
+
+    def finish(total, lo):
+        total = total * (1.0 / (CHIPS_Z * CHIPS_Y * CORES))
+        width = total.shape[1]
+        gate_out[:, lo : lo + width] = total[:32]
+        down_out[:, lo : lo + width] = total[32:40]
+        down_out[:, WIDTH + lo : WIDTH + lo + width] = total[40:48]
+
+    def a_end():
+        total = wide(own_a[z, y])
+        for side in range(2):
+            copies["ay", side, 2].wait_recv()
+            total = total + wide(ay_buf[side, 1])
+        finish(total, 0)
+
+    def b_y(side, step, piece, received):
+        off = (3 - step) if side == 0 else step - 3
+        at_z = zi(piece)
+        slot = ORDER_Z.index(piece)
+        if received:
+            copies["by", side, step - 1, piece].wait_recv()
+            add_into(own_b, (yi(off), at_z), by_buf[side, step - 2, slot])
+        copies["by", side, step, piece] = send(
+            own_b.at[yi(off), at_z], by_buf.at[side, step - 1, slot], by_sem, (side, step - 1, slot),
+            y_next if side == 0 else y_prev,
+        )
+
+    def b_y_end(piece):
+        total = wide(own_b[y, zi(piece)])
+        for side in range(2):
+            copies["by", side, 2, piece].wait_recv()
+            total = total + wide(by_buf[side, 1, ORDER_Z.index(piece)])
+        own_b[y, zi(piece)] = total.astype(jnp.bfloat16)
+
+    def b_z(side, step):
+        off = (5 - step) if side == 0 else step - 5
+        rows = half_rows["bz", side] if step == 1 else slice(0, 48)
+        if step > 1:
+            before = half_rows["bz", side] if step == 2 else slice(0, 48)
+            copies["bz", side, step - 1].wait_recv()
+            add_into(own_b, (y, zi(off), before), bz_buf[side, step - 2, before])
+        copies["bz", side, step] = send(
+            own_b.at[y, zi(off), rows], bz_buf.at[side, step - 1, rows], bz_sem, (side, step - 1),
+            z_next if side == 0 else z_prev,
+        )
+
+    def b_end():
+        total = wide(own_b[y, z])
+        for side in range(2):
+            copies["bz", side, 4].wait_recv()
+            total = total + wide(bz_buf[side, 3])
+        finish(total, COLS_A)
+
+    upper, lower = (4, 3, 2, 1), (-3, -2, -1, 0)
+    first = {0: (0, 1), 1: (2, 3)}
+    early_b = {0: upper, 1: lower}
+
+    give_group_a(4)
+    give_group_a(3)
+    give_group_a(-3)
+    give_group_b(2)
+    give_group_b(1)
+    give_group_b(-1)
+    take_group_a(4)
+    for piece in range(2):
+        for side in range(2):
+            a_z(side, 1, first[side][piece], False)
+    give_group_a(2)
+    give_group_a(-2)
+    take_group_a(3)
+    take_group_a(-3)
+    for piece in range(2):
+        for side in range(2):
+            a_z(side, 2, first[1 - side][piece], False)
+    take_group_b(2)
+    for piece in range(4):
+        for side in range(2):
+            b_y(side, 1, early_b[side][piece], False)
+    give_group_b(0)
+    give_group_a(1)
+    give_group_a(-1)
+    give_group_a(0)
+    take_group_b(1)
+    take_group_b(-1)
+    for piece in range(4):
+        for side in range(2):
+            b_y(side, 2, early_b[1 - side][piece], False)
+    for piece in range(2):
+        for side in range(2):
+            a_z(side, 2, first[side][piece], True)
+    take_group_a(2)
+    take_group_a(-2)
+    for piece in range(2):
+        for side in range(2):
+            a_z(side, 3, first[1 - side][piece], True)
+    for piece in range(2):
+        for side in range(2):
+            b_y(side, 2, early_b[side][piece], True)
+    take_group_a(1)
+    take_group_a(-1)
+    for piece in range(2):
+        for side in range(2):
+            a_z(side, 3, first[side][piece], True)
+    for piece in range(2, 4):
+        for side in range(2):
+            b_y(side, 2, early_b[side][piece], True)
+    take_group_b(0)
+    take_group_a(0)
+    for piece in range(2):
+        for side in range(2):
+            a_z(side, 4, first[1 - side][piece], True)
+    b_y_end(4)
+    for side in range(2):
+        b_z(side, 1)
+    for piece in range(2):
+        for side in range(2):
+            a_z(side, 4, first[side][piece], True)
+    b_y_end(3)
+    b_y_end(-3)
+    for side in range(2):
+        b_z(side, 2)
+    b_y_end(2)
+    b_y_end(-2)
+    for side in range(2):
+        b_z(side, 3)
+    b_y_end(1)
+    b_y_end(-1)
+    b_y_end(0)
+    for yy in (2, 3, 0, 1):
+        a_z_end(yy)
+    for side in range(2):
+        a_y(side, 1)
+    for side in range(2):
+        b_z(side, 4)
+    for side in range(2):
+        a_y(side, 2)
+    b_end()
+    a_end()
+    for copy in started:
+        copy.wait_send()
+
+
+def reduce_scatter(gate_up_term, down_term):
+    bf16 = jnp.bfloat16
+    sems = pltpu.SemaphoreType.DMA
+    vmem = pl.BlockSpec(memory_space=pltpu.VMEM)
+    return pl.pallas_call(
+        scatter_kernel,
+        out_shape=(
+            jax.ShapeDtypeStruct((GATE_ROWS, WIDTH), jnp.float32),
+            jax.ShapeDtypeStruct((DOWN_ROWS, 2 * WIDTH), jnp.float32),
+        ),
+        in_specs=[vmem, vmem],
+        out_specs=(vmem, vmem),
+        scratch_shapes=[
+            pltpu.VMEM((CHIPS_Z, CHIPS_Y, SHARE, COLS_A), bf16),
+            pltpu.VMEM((CHIPS_Y, CHIPS_Z, SHARE, COLS_B), bf16),
+            pltpu.VMEM((CHIPS_Z, CHIPS_Y, SHARE, COLS_A), bf16),
+            pltpu.VMEM((CHIPS_Y, CHIPS_Z, SHARE, COLS_B), bf16),
+            pltpu.VMEM((CHIPS_Z, CHIPS_Y, SHARE, COLS_A), bf16),
+            pltpu.VMEM((CHIPS_Y, CHIPS_Z, SHARE, COLS_B), bf16),
+            pltpu.VMEM((2, 4, CHIPS_Y, SHARE, COLS_A), bf16),
+            pltpu.VMEM((2, 2, SHARE, COLS_A), bf16),
+            pltpu.VMEM((2, 2, CHIPS_Z, SHARE, COLS_B), bf16),
+            pltpu.VMEM((2, 4, SHARE, COLS_B), bf16),
+            sems((2, 8)),
+            sems((2, 4)),
+            sems((2, 2, 4, 4)),
+            sems((2, 2, 2)),
+            sems((2, 2, 2, 8)),
+            sems((2, 2, 4)),
+        ],
+        compiler_params=pltpu.CompilerParams(
+            collective_id=0, has_side_effects=True, vmem_limit_bytes=60 * 1024 * 1024
+        ),
+    )(gate_up_term, down_term)
 
 
 def expert_forward(token_rows, gate_up):
@@ -80,17 +401,10 @@
     returned = returned.reshape(total_rows, model_width)
     pick_rows = expert_ids * capacity + jnp.take_along_axis(slot_index, expert_ids, axis=1)
     token_grad = jnp.sum(returned[pick_rows].astype(jnp.float32), axis=1).astype(jnp.bfloat16)
-    gate_up_round = gate_up_term.astype(jnp.bfloat16)
-    down_round = (down_term + down_residual[0, 0].astype(jnp.float32)).astype(jnp.bfloat16)
-    group_count = lax.axis_size("dp")
-    gate_up_wide = lax.optimization_barrier(gate_up_round).astype(jnp.float32)
-    down_wide = lax.optimization_barrier(down_round).astype(jnp.float32)
-    gate_up_part, down_part = (
-        lax.psum_scatter(gate_up_wide, "dp", scatter_dimension=0, tiled=True),
-        lax.psum_scatter(down_wide, "dp", scatter_dimension=0, tiled=True),
-    )
-    factor = 1.0 / group_count
-    return (token_grad, (gate_up_part * factor)[None], (down_part * factor)[None])
+    gate_up_part, down_part = reduce_scatter(
+        gate_up_term, down_term + down_residual[0, 0].astype(jnp.float32)
+    )
+    return (token_grad, gate_up_part[None], down_part[None])
 
 
 def solution(mesh):

time: 403 us -> 123 us (0.31)
  blocking collectives: 303 us -> 0 us
  Pallas kernels: 0 us -> 45.8 us
  between operations: 14.9 us -> 0.85 us
  other arithmetic: 15.2 us -> 7.89 us
  matrix products: 18.8 us -> 23.4 us
    unnamed x1 -> x0, blocking collectives: 303 us -> none
    pallas_call x0 -> x1, Pallas kernels: none -> 45.8 us  [reduce_scatter(): pl.pallas_call(scatter_kernel, out_shape=(jax.ShapeDtypeStruct((GATE_ROWS...]
    convert_element_type x1 -> x0, other arithmetic: 4.26 us -> none  [on_device(): gate_up_wide = lax.optimization_barrier(gate_up_round).astype(jnp.float32)]
  transfers between devices with their start and end apart: 4 -> 3, of which waited for: 2 -> 2; matrix products, arithmetic and copies ran while one was open for 8% -> 22% of each run, Pallas kernels for 0% -> 38%
where the time goes in v1:
time: 123 us; the launch traced here: 121 us
  Pallas kernels  45.8 us (37%)
  matrix products  23.4 us (19%)
  local copies, waits for them, and re-layouts  16.1 us (13%)
  waiting for transfers between devices  15.2 us (12%)
  starting transfers between devices  12.2 us (10%)
  other arithmetic  7.89 us (6%)
    pallas_call x1, Pallas kernels, reduce_scatter(): pl.pallas_call(scatter_kernel, out_shape=(jax.ShapeDtypeStruct((GATE_ROWS...  45.8 us
    all_to_all x1, waiting for transfers between devices, on_device(): lax.all_to_all(send_rows, 'expert', split_axis=0, concat_axis=0, tiled=True)  9.5 us
    dot_general x1, matrix products, expert_backward(): lax.dot_general(token_rows, back_both, contract, preferred_element_type=j...  6.91 us
    dot_general x1, matrix products, expert_backward(): lax.dot_general(hidden, scaled, contract, preferred_element_type=jnp.floa...  5.76 us
    all_to_all x1, waiting for transfers between devices, on_device(): lax.all_to_all(send_grads, 'expert', split_axis=0, concat_axis=0, tiled=T...  5.72 us
    dot_general x1, matrix products, expert_forward(): projected = jnp.dot(token_rows, gate_up, preferred_element_type=jnp.float32)  5.19 us
    all_to_all x1, starting transfers between devices, on_device(): lax.all_to_all(send_rows, 'expert', split_axis=0, concat_axis=0, tiled=True)  4.97 us
    gather x2, local copies, waits for them, and re-layouts, on_device(): returned[pick_rows].astype(jnp.float32)  4.09 us
  transfers between devices with their start and end apart: 3, of which 2 were waited for; matrix products, arithmetic and copies ran while one was open for 22% of the time, Pallas kernels for 38%

profile of v1, /device:TPU:1, one launch (start us, length us, event | category | flops | bytes accessed | tf_op | source)
XLA Modules:
  0.0 121.4 jit_solution(1251513261539636283)
XLA Ops:
  0.6 0.8 fusion.15
  1.6 0.2 reduce_window_sum.11
  1.9 0.2 fusion.13
  2.0 0.2 select_reduce_fusion.1
  2.3 1.1 concatenate.11
  3.4 3.0 %gather_fusion.1 = bf16[320,2048]{1,0:T(8,128)(2,1)} fusion(bf16[129,2048]{1,0:T(8,128)(2,1)S(1)} %concatenate.11, s32[1024]{0:T(1024)S(1)} %pad_clamp_fusion.1), kind=kCustom, calls=%fused_computation.1 | custom fusion | bytes 2622720 | tf_op jit(solution)/shard_map/gather | solution.py:376
  6.4 5.0 %all-to-all-start.1 = ((bf16[4,80,2048]{2,1,0:T(8,128)(2,1)}), bf16[4,80,2048]{2,1,0:T(8,128)(2,1)}, u32[]{:S(2)}, u32[]{:S(2)}) async-start(bf16[4,80,2048]{2,1,0:T(8,128)(2,1)} %bitcast.46), calls=%async_computation.1 | async-start | bytes 2621440 | tf_op jit(solution)/shard_map/all_to_all | solution.py:385
  11.5 3.0 %gather_fusion = bf16[320,2048]{1,0:T(8,128)(2,1)} fusion(bf16[129,2048]{1,0:T(8,128)(2,1)S(1)} %concatenate.10, s32[1024]{0:T(1024)S(1)} %pad_clamp_fusion.1), kind=kCustom, calls=%fused_computation | custom fusion | bytes 2622720 | tf_op jit(solution)/shard_map/gather | solution.py:378
  14.5 0.1 select_reduce_fusion
  14.6 2.7 %fusion.7 = bf16[4,80,2048]{2,1,0:T(8,128)(2,1)} fusion(bf16[4,80,2048]{2,1,0:T(8,128)(2,1)} %bitcast.47, f32[4,80]{1,0:T(4,128)S(1)} %select_reduce_fusion), kind=kLoop, calls=%fused_computation.11 | loop fusion | flops 1966080 | bytes 2622720 | tf_op jit(solution)/shard_map/convert_element_type | solution.py:380
  17.3 9.5 %all-to-all-done.1 = bf16[4,80,2048]{2,1,0:T(8,128)(2,1)} async-done(((bf16[4,80,2048]{2,1,0:T(8,128)(2,1)}), bf16[4,80,2048]{2,1,0:T(8,128)(2,1)}, u32[]{:S(2)}, u32[]{:S(2)}) %all-to-all-start.1) | async-done | bytes 1310752 | tf_op jit(solution)/shard_map/all_to_all | solution.py:385
  26.8 3.5 %all-to-all-start = ((bf16[4,80,2048]{2,1,0:T(8,128)(2,1)}), bf16[4,80,2048]{2,1,0:T(8,128)(2,1)S(1)}, u32[]{:S(2)}, u32[]{:S(2)}) async-start(bf16[4,80,2048]{2,1,0:T(8,128)(2,1)} %fusion.7), calls=%async_computation | async-start | bytes 2621440 | tf_op jit(solution)/shard_map/all_to_all | solution.py:386
  30.4 0.1 copy.46
  30.5 0.1 reshape.88
  30.6 2.4 %gather_fusion.3 = s32[256]{0:T(256)S(1)} fusion(s32[128,4]{0,1:T(4,128)S(1)} %convert_subtract_fusion, s32[256]{0:T(256)S(1)} %reshape.88), kind=kCustom, calls=%fused_computation.3 | custom fusion | bytes 4096 | tf_op jit(solution)/shard_map/jit(take_along_axis)/gather | solution.py:402
  33.0 0.1 reshape.91
  33.2 0.1 copy.48
  33.4 0.1 reshape.82
  33.5 5.2 %fusion.2 = f32[320,1024]{1,0:T(8,128)} fusion(bf16[320,2048]{1,0:T(8,128)(2,1)} %bitcast.8, bf16[1,2048,1024]{2,1,0:T(8,128)(2,1)} %param.11), kind=kOutput, calls=%fused_computation.7 | convolution fusion | flops 1342177280 | bytes 6815744 | tf_op jit(solution)/shard_map/dot_general | solution.py:330
  38.7 5.7 %all-to-all-done = bf16[4,80,2048]{2,1,0:T(8,128)(2,1)S(1)} async-done(((bf16[4,80,2048]{2,1,0:T(8,128)(2,1)}), bf16[4,80,2048]{2,1,0:T(8,128)(2,1)S(1)}, u32[]{:S(2)}, u32[]{:S(2)}) %all-to-all-start) | async-done | bytes 1310752 | tf_op jit(solution)/shard_map/all_to_all | solution.py:386
  44.4 2.9 %multiply_convert_fusion.2 = (bf16[320,512]{1,0:T(8,128)(2,1)S(1)}, bf16[320,512]{1,0:T(8,128)(2,1)S(1)}) fusion(f32[320,1024]{1,0:T(8,128)} %fusion.2, bf16[320,2048]{1,0:T(8,128)(2,1)S(1)} %bitcast.44, bf16[1,512,2048]{2,1,0:T(8,128)(2,1)S(1)} %copy-done), kind=kOutput, calls=%fused_computation.17 | convolution fusion | flops 673218560 | bytes 5373952 | tf_op jit(solution)/shard_map/dot_general | solution.py:341
  47.4 0.1 copy-done.11
  47.5 2.6 %fusion.4 = bf16[320,2048]{1,0:T(8,128)(2,1)} fusion(bf16[1,2048,1024]{2,1,0:T(8,128)(2,1)S(1)} %copy-done.11, bf16[320,512]{1,0:T(8,128)(2,1)S(1)} %get-tuple-element.8, bf16[320,512]{1,0:T(8,128)(2,1)S(1)} %get-tuple-element.7), kind=kOutput, calls=%fused_computation.9 | convolution fusion | flops 1344143360 | bytes 6160384 | tf_op jit(solution)/shard_map/dot_general | solution.py:345
  50.1 3.7 %all-to-all-start.2 = ((bf16[4,80,2048]{2,1,0:T(8,128)(2,1)}), bf16[4,80,2048]{2,1,0:T(8,128)(2,1)S(1)}, u32[]{:S(2)}, u32[]{:S(2)}) async-start(bf16[4,80,2048]{2,1,0:T(8,128)(2,1)} %bitcast.48), calls=%async_computation.2 | async-start | bytes 2621440 | tf_op jit(solution)/shard_map/all_to_all | solution.py:394
  53.9 5.8 %convert_add_fusion.down_ref = f32[512,2048]{1,0:T(8,128)} fusion(bf16[320,2048]{1,0:T(8,128)(2,1)} %bitcast.45, bf16[1,1,512,2048]{3,2,1,0:T(8,128)(2,1)} %param.13, f32[320,1024]{1,0:T(8,128)} %fusion.2), kind=kOutput, calls=%fused_computation.4 | convolution fusion | flops 674168832 | bytes 8912896 | tf_op jit(solution)/shard_map/dot_general | solution.py:352
  59.7 6.9 %fusion.11.gate_ref = f32[2048,1024]{1,0:T(8,128)} fusion(bf16[320,2048]{1,0:T(8,128)(2,1)} %bitcast.8, bf16[320,512]{1,0:T(8,128)(2,1)S(1)} %copy-done.6, bf16[320,512]{1,0:T(8,128)(2,1)S(1)} %copy-done.4), kind=kOutput, calls=%fused_computation.20 | convolution fusion | flops 1343488000 | bytes 10354688 | tf_op jit(solution)/shard_map/dot_general | solution.py:349
  66.6 45.8 %shard_map.94 = (f32[32,1024]{1,0:T(8,128)}, f32[8,2048]{1,0:T(8,128)}) custom-call(f32[2048,1024]{1,0:T(8,128)} %fusion.11.gate_ref, f32[512,2048]{1,0:T(8,128)} %convert_add_fusion.down_ref), custom_call_target="tpu_custom_call" | custom-call | tf_op jit(solution)/shard_map/pallas_call | solution.py:296
  112.4 2.3 %gather_fusion.2 = bf16[256,2048]{1,0:T(8,128)(2,1)} fusion(bf16[320,2048]{1,0:T(8,128)(2,1)S(1)} %bitcast.43, s32[1024]{0:T(1024)S(1)} %pad_clamp_fusion), kind=kCustom, calls=%fused_computation.2 | custom fusion | bytes 2098176 | tf_op jit(solution)/shard_map/gather | solution.py:403
  114.7 1.7 %reshape.85 = bf16[128,2,2048]{2,1,0:T(2,128)(2,1)S(1)} reshape(bf16[256,2048]{1,0:T(8,128)(2,1)} %gather_fusion.2) | data formatting | bytes 2097152 | tf_op jit(solution)/shard_map/gather | solution.py:403
  116.5 3.6 %reduce_sum.42 = bf16[128,2048]{1,0:T(8,128)(2,1)} reduce(bf16[128,2,2048]{2,1,0:T(2,128)(2,1)S(1)} %reshape.85, bf16[]{:T(256)} %constant.9.clone.1), dimensions={1}, to_apply=%region_6.7 | reduce | flops 262144 | bytes 1572866 | tf_op jit(solution)/shard_map/reduce_sum | solution.py:403
  120.1 0.7 copy.51
  120.8 0.6 copy.52
  (37 shorter events, 0.5 us)
Async XLA Ops:
  0.6 43.8 %copy-start = (bf16[1,512,2048]{2,1,0:T(8,128)(2,1)S(1)}, bf16[1,512,2048]{2,1,0:T(8,128)(2,1)}, u32[]{:S(2)}) copy-start(bf16[1,512,2048]{2,1,0:T(8,128)(2,1)} %param.12) | copy-start | bytes 6291460
  6.4 5.0 %copy-start.2 = (bf16[128,2048]{1,0:T(8,128)(2,1)S(1)}, bf16[128,2048]{1,0:T(8,128)(2,1)}, u32[]{:S(2)}) copy-start(bf16[128,2048]{1,0:T(8,128)(2,1)} %param.8) | copy-start | bytes 1572868
  6.4 20.4 %all-to-all-start.1 = ((bf16[4,80,2048]{2,1,0:T(8,128)(2,1)}), bf16[4,80,2048]{2,1,0:T(8,128)(2,1)}, u32[]{:S(2)}, u32[]{:S(2)}) async-start(bf16[4,80,2048]{2,1,0:T(8,128)(2,1)} %bitcast.46), calls=%async_computation.1 | async-start | bytes 2621440 | tf_op jit(solution)/shard_map/all_to_all | solution.py:385
  11.4 3.0 %copy-start.9 = (s32[128,2]{0,1:T(2,128)S(1)}, s32[128,2]{0,1:T(2,128)}, u32[]{:S(2)}) copy-start(s32[128,2]{0,1:T(2,128)} %param.9) | copy-start | bytes 3076
  11.4 3.0 %copy-start.10 = (f32[128,2]{0,1:T(2,128)S(1)}, f32[128,2]{0,1:T(2,128)}, u32[]{:S(2)}) copy-start(f32[128,2]{0,1:T(2,128)} %param.10) | copy-start | bytes 3076
  26.8 17.6 %all-to-all-start = ((bf16[4,80,2048]{2,1,0:T(8,128)(2,1)}), bf16[4,80,2048]{2,1,0:T(8,128)(2,1)S(1)}, u32[]{:S(2)}, u32[]{:S(2)}) async-start(bf16[4,80,2048]{2,1,0:T(8,128)(2,1)} %fusion.7), calls=%async_computation | async-start | bytes 2621440 | tf_op jit(solution)/shard_map/all_to_all | solution.py:386
  44.4 2.9 %copy-start.1 = (bf16[4,80,2048]{2,1,0:T(8,128)(2,1)}, bf16[4,80,2048]{2,1,0:T(8,128)(2,1)S(1)}, u32[]{:S(2)}) copy-start(bf16[4,80,2048]{2,1,0:T(8,128)(2,1)S(1)} %all-to-all-done) | copy-start | bytes 3932164
  44.4 3.1 %copy-start.11 = (bf16[1,2048,1024]{2,1,0:T(8,128)(2,1)S(1)}, bf16[1,2048,1024]{2,1,0:T(8,128)(2,1)}, u32[]{:S(2)}) copy-start(bf16[1,2048,1024]{2,1,0:T(8,128)(2,1)} %param.11) | copy-start | bytes 12582916
  47.4 2.8 %copy-start.3 = (bf16[320,512]{1,0:T(8,128)(2,1)}, bf16[320,512]{1,0:T(8,128)(2,1)S(1)}, u32[]{:S(2)}) copy-start(bf16[320,512]{1,0:T(8,128)(2,1)S(1)} %get-tuple-element.7) | copy-start | bytes 983044
  47.4 2.8 %copy-start.5 = (bf16[320,512]{1,0:T(8,128)(2,1)}, bf16[320,512]{1,0:T(8,128)(2,1)S(1)}, u32[]{:S(2)}) copy-start(bf16[320,512]{1,0:T(8,128)(2,1)S(1)} %get-tuple-element.8) | copy-start | bytes 983044
  50.1 62.3 %all-to-all-start.2 = ((bf16[4,80,2048]{2,1,0:T(8,128)(2,1)}), bf16[4,80,2048]{2,1,0:T(8,128)(2,1)S(1)}, u32[]{:S(2)}, u32[]{:S(2)}) async-start(bf16[4,80,2048]{2,1,0:T(8,128)(2,1)} %bitcast.48), calls=%async_computation.2 | async-start | bytes 2621440 | tf_op jit(solution)/shard_map/all_to_all | solution.py:394
  53.9 5.8 %copy-start.4 = (bf16[320,512]{1,0:T(8,128)(2,1)S(1)}, bf16[320,512]{1,0:T(8,128)(2,1)}, u32[]{:S(2)}) copy-start(bf16[320,512]{1,0:T(8,128)(2,1)} %copy-done.3) | copy-start | bytes 983044
  53.9 5.8 %copy-start.6 = (bf16[320,512]{1,0:T(8,128)(2,1)S(1)}, bf16[320,512]{1,0:T(8,128)(2,1)}, u32[]{:S(2)}) copy-start(bf16[320,512]{1,0:T(8,128)(2,1)} %copy-done.5) | copy-start | bytes 983044
  116.5 3.7 %copy-start.7 = (f32[32,1024]{1,0:T(8,128)S(1)}, f32[32,1024]{1,0:T(8,128)}, u32[]{:S(2)}) copy-start(f32[32,1024]{1,0:T(8,128)} %get-tuple-element.5) | copy-start | bytes 393220
  116.5 4.3 %copy-start.8 = (f32[8,2048]{1,0:T(8,128)S(1)}, f32[8,2048]{1,0:T(8,128)}, u32[]{:S(2)}) copy-start(f32[8,2048]{1,0:T(8,128)} %get-tuple-element.6) | copy-start | bytes 196612

commit v2 on v0

v2 whole, which is shorter than its diff:
```python
import jax
import jax.numpy as jnp
from jax import lax
from jax.experimental import pallas as pl
from jax.experimental.pallas import tpu as pltpu
from jax.sharding import PartitionSpec as P

MESH = pl.DeviceIdType.MESH
CHIPS_Z, CHIPS_Y, CORES, EXPERTS = 8, 4, 2, 4
SHARE = 48
GATE_ROWS, DOWN_ROWS = 32, 8
WIDTH = 1024
COLS_A = 512
COLS_B = WIDTH - COLS_A
ORDER_Z = (4, 3, -3, 2, -2, 1, -1, 0)
ORDER_Y = (2, 1, -1, 0)
TOK, CAP, MODEL, UNITS = 128, 80, 2048, 512
ROWS = EXPERTS * CAP
OPP, SELF, LOW, HIGH = (slice(k * CAP, (k + 1) * CAP) for k in range(4))
EARLY, LATE, NEAR = slice(0, 2 * CAP), slice(2 * CAP, ROWS), slice(CAP, ROWS)


def wide(value):
    return value.astype(jnp.float32)


def dot(left, right):
    return jnp.dot(left, right, preferred_element_type=jnp.float32)


def dot_rows(left, right):
    return lax.dot_general(left, right, (((0,), (0,)), ((), ())), preferred_element_type=jnp.float32)


def columns(index, width):
    return pl.ds(pl.multiple_of(index * width, width), width)


def loop(count, body):
    def step(index, carry):
        body(index)
        return carry

    lax.fori_loop(0, count, step, 0)


def layer_kernel(
    ids_ref, probs_ref, tokens_hbm, cotangent_hbm, gate_up_hbm, down_hbm, residual_hbm,
    token_out, gate_out, down_out,
    tok_in, cot_in, gate_up, down, residual, gate_up_t, down_t,
    place, slot_weight, tok_send, grad_send, tok_relay, grad_relay,
    tok_all, grad_all, both, back, hidden, sum_gate, sum_down,
    part, part_relay, returned,
    half_a, half_b, got_a, got_b, az_buf, ay_buf, by_buf, bz_buf,
    load_sem, swap_sem, return_sem,
    pair_a_sem, pair_b_sem, az_sem, ay_sem, by_sem, bz_sem,
):
    bf16 = jnp.bfloat16
    me, x = lax.axis_index("dp"), lax.axis_index("expert")
    z, y, core = me // (CHIPS_Y * CORES), (me // CORES) % CHIPS_Y, me % CORES

    def at(zz, yy, cc):
        return (((zz + CHIPS_Z) % CHIPS_Z) * CHIPS_Y + (yy + CHIPS_Y) % CHIPS_Y) * CORES + cc

    def zi(off):
        return (z + off + CHIPS_Z) % CHIPS_Z

    def yi(off):
        return (y + off + CHIPS_Y) % CHIPS_Y

    partner = (at(z, y, 1 - core), x)
    z_side = ((at(z + 1, y, core), x), (at(z - 1, y, core), x))
    y_side = ((at(z, y + 1, core), x), (at(z, y - 1, core), x))
    x_side = ((me, (x + 1) % EXPERTS), (me, (x + EXPERTS - 1) % EXPERTS))
    barrier = pltpu.get_barrier_semaphore()
    for device in (partner, *z_side, *y_side, *x_side):
        pl.semaphore_signal(barrier, inc=1, device_id=device, device_id_type=MESH)

    loads = [
        pltpu.make_async_copy(source, target, load_sem.at[k])
        for k, (source, target) in enumerate(
            (
                (tokens_hbm, tok_in),
                (cotangent_hbm, cot_in),
                (down_hbm, down),
                (gate_up_hbm, gate_up),
                (residual_hbm, residual),
            )
        )
    ]
    for copy in loads:
        copy.start()

    started = []

    def send(src, dst, sems, index, device):
        copy = pltpu.make_async_remote_copy(
            src_ref=src, dst_ref=dst, send_sem=sems.at[(0, *index)], recv_sem=sems.at[(1, *index)],
            device_id=device, device_id_type=MESH,
        )
        copy.start()
        started.append(copy)
        return copy

    ids, probs = ids_ref[...], probs_ref[...]
    before = lax.broadcasted_iota(jnp.int32, (TOK, TOK), 0) < lax.broadcasted_iota(jnp.int32, (TOK, TOK), 1)
    before = jnp.where(before, 1.0, 0.0).astype(bf16)
    slots = wide(lax.broadcasted_iota(jnp.int32, (CAP, TOK), 0))
    for k in range(EXPERTS):
        expert = (x + k) % EXPERTS
        hits = ids == expert
        member = jnp.sum(jnp.where(hits, 1.0, 0.0), axis=0, keepdims=True)
        weight = jnp.sum(jnp.where(hits, probs, 0.0), axis=0, keepdims=True)
        index = dot(jnp.broadcast_to(member, (8, TOK)).astype(bf16), before)[0:1]
        chosen = jnp.where((slots == index) & (member > 0.5), 1.0, 0.0)
        rows = slice(k * CAP, (k + 1) * CAP)
        place[rows] = chosen.astype(bf16)
        slot_weight[rows] = jnp.broadcast_to(jnp.sum(chosen * weight, axis=1, keepdims=True), (CAP, TOK))

    def pick_tokens(k, target, rows):
        def body(n):
            cols = columns(n, 512)
            target[rows, cols] = dot(place[k * CAP : (k + 1) * CAP], tok_in[:, cols]).astype(bf16)
        loop(4, body)

    def pick_grads(k, target, rows):
        def body(n):
            cols = columns(n, 512)
            block = slice(k * CAP, (k + 1) * CAP)
            value = dot(place[block], cot_in[:, cols]) * slot_weight[block, 0:1]
            target[rows, cols] = value.astype(bf16)
        loop(4, body)

    swap = {}
    first, second, third = slice(0, CAP), slice(CAP, 2 * CAP), slice(2 * CAP, 3 * CAP)
    loads[0].wait()
    pick_tokens(2, tok_send, second)
    pl.semaphore_wait(barrier, 7)
    swap["tok", "leg"] = send(tok_send.at[second], tok_relay, swap_sem, (0,), x_side[0])
    loads[1].wait()
    pick_grads(2, grad_send, second)
    swap["grad", "leg"] = send(grad_send.at[second], grad_relay, swap_sem, (1,), x_side[1])
    pick_tokens(1, tok_send, first)
    swap["tok", 0] = send(tok_send.at[first], tok_all.at[LOW], swap_sem, (2,), x_side[0])
    pick_tokens(3, tok_send, third)
    swap["tok", 1] = send(tok_send.at[third], tok_all.at[HIGH], swap_sem, (3,), x_side[1])
    pick_grads(1, grad_send, first)
    pick_grads(3, grad_send, third)
    pick_tokens(0, tok_all, SELF)
    pick_grads(0, grad_all, SELF)
    loads[2].wait()

    def turn_down(n):
        rows = columns(n, 256)
        down_t[rows, :] = down[:, rows].T

    loop(8, turn_down)
    swap["tok", "leg"].wait_recv()
    swap["tok", "far"] = send(tok_relay, tok_all.at[OPP], swap_sem, (4,), x_side[0])
    swap["grad", "leg"].wait_recv()
    swap["grad", "far"] = send(grad_relay, grad_all.at[OPP], swap_sem, (5,), x_side[1])
    swap["grad", 0] = send(grad_send.at[first], grad_all.at[LOW], swap_sem, (6,), x_side[0])
    swap["grad", 1] = send(grad_send.at[third], grad_all.at[HIGH], swap_sem, (7,), x_side[1])
    loads[3].wait()

    def turn_gate_up(n):
        rows = columns(n, 256)
        gate_up_t[:, rows] = gate_up[rows, :].T

    loop(8, turn_gate_up)
    loads[4].wait()

    def project(rows):
        def body(n):
            cols = columns(n, 256)
            both[rows, cols] = dot(tok_all[rows], gate_up[:, cols])
        loop(4, body)

        def gates(n):
            r = pl.ds(pl.multiple_of(rows.start + n * 16, 16), 16)
            gate, up = both[r, 0:UNITS], both[r, UNITS : 2 * UNITS]
            sig = jax.nn.sigmoid(gate)
            active = gate * sig
            hidden[r] = (active * up).astype(bf16)
            both[r, 0:UNITS] = up * sig * (1.0 + gate * (1.0 - sig))
            both[r, UNITS : 2 * UNITS] = active
        loop((rows.stop - rows.start) // 16, gates)

    def pull_back(rows):
        def body(n):
            cols, upper = columns(n, 256), columns(n + 2, 256)
            value = dot(grad_all[rows], down_t[:, cols])
            back[rows, cols] = (value * both[rows, cols]).astype(bf16)
            back[rows, upper] = (value * both[rows, upper]).astype(bf16)
        loop(2, body)

    swap["tok", 0].wait_recv()
    swap["tok", 1].wait_recv()
    project(NEAR)
    swap["tok", "far"].wait_recv()
    project(OPP)
    swap["grad", "far"].wait_recv()
    pull_back(EARLY)

    def early_gate(n):
        rows = columns(n, 256)
        turned = tok_all[EARLY, rows].T
        for half in range(2):
            cols = slice(half * 512, half * 512 + 512)
            sum_gate[rows, cols] = dot(turned, back[EARLY, cols])
    loop(8, early_gate)

    def early_down(n):
        rows = columns(n, 128)
        turned = hidden[EARLY, rows].T
        for half in range(4):
            cols = slice(half * 512, half * 512 + 512)
            sum_down[rows, cols] = dot(turned, grad_all[EARLY, cols]) + wide(residual[rows, cols])
    loop(4, early_down)

    swap["grad", 0].wait_recv()
    swap["grad", 1].wait_recv()
    pull_back(LATE)

    def late_down(n):
        rows = columns(n, 128)
        turned = hidden[LATE, rows].T
        for half in range(4):
            cols = slice(half * 512, half * 512 + 512)
            sum_down[rows, cols] += dot(turned, grad_all[LATE, cols])
    loop(4, late_down)

    def pair_a(k, zz):
        return pltpu.make_async_remote_copy(
            src_ref=half_a.at[1 - core, zz], dst_ref=got_a.at[zz],
            send_sem=pair_a_sem.at[0, k], recv_sem=pair_a_sem.at[1, k],
            device_id=partner, device_id_type=MESH,
        )

    def late_gate(k):
        zz = (z + 4 + ((k + 1) // 2) * (1 - 2 * ((k + 1) % 2)) + CHIPS_Z) % CHIPS_Z
        rows = columns(zz, 256)
        turned = tok_all[LATE, rows].T
        down_rows = [
            pl.ds(pl.multiple_of(zz * 64 + part_at * 8, 8), 8) for part_at in range(8)
        ]
        for half, lo in ((half_a, 0), (half_b, COLS_A)):
            hi = lo + (COLS_A if half is half_a else COLS_B)
            value = sum_gate[rows, lo:hi] + dot(turned, back[LATE, lo:hi])
            for yy in range(CHIPS_Y):
                for cc in range(CORES):
                    index = yy * CORES + cc
                    slot = (cc, zz, yy) if half is half_a else (cc, yy, zz)
                    half[(*slot, slice(0, 32))] = value[32 * index : 32 * index + 32].astype(bf16)
                    low = jnp.concatenate(
                        [
                            sum_down[down_rows[index], lo:hi],
                            sum_down[down_rows[index], WIDTH + lo : WIDTH + hi],
                        ],
                        axis=0,
                    )
                    half[(*slot, slice(32, 48))] = low.astype(bf16)
        pair_a(k, zz).start()

    loop(8, late_gate)
    pair_copies = {("a", off): pair_a(ORDER_PAIR.index(off), zi(off)) for off in ORDER_Z}
    started.extend(pair_copies.values())
    for off in ORDER_Y:
        pair_copies["b", off] = send(
            half_b.at[1 - core, yi(off)], got_b.at[yi(off)], pair_b_sem, (ORDER_Y.index(off),), partner
        )
    own_a, own_b = half_a.at[core], half_b.at[core]

    def take_group_a(off):
        pair_copies["a", off].wait_recv()

        def body(yy):
            own_a[zi(off), yy] = (wide(own_a[zi(off), yy]) + wide(got_a[zi(off), yy])).astype(bf16)
        loop(CHIPS_Y, body)

    def take_group_b(off):
        pair_copies["b", off].wait_recv()

        def body(zz):
            own_b[yi(off), zz] = (wide(own_b[yi(off), zz]) + wide(got_b[yi(off), zz])).astype(bf16)
        loop(CHIPS_Z, body)

    back_copies = {}

    def token_columns(n):
        cols = slice(n * 256, n * 256 + 256)
        value = dot(back[...], gate_up_t[:, cols]).astype(bf16)
        part[:, cols] = value
        returned[0:CAP, cols] = value[SELF]

    def give_back(half):
        cols = slice(half * 1024, half * 1024 + 1024)
        other = x_side[half]
        back_copies["high", half] = send(
            part.at[HIGH, cols], returned.at[3 * CAP : 4 * CAP, cols], return_sem, (half, 0), x_side[0]
        )
        back_copies["low", half] = send(
            part.at[LOW, cols], returned.at[CAP : 2 * CAP, cols], return_sem, (half, 1), x_side[1]
        )
        back_copies["leg", half] = send(
            part.at[OPP, cols], part_relay.at[half], return_sem, (half, 2), other
        )

    def pass_on(half):
        cols = slice(half * 1024, half * 1024 + 1024)
        back_copies["leg", half].wait_recv()
        back_copies["far", half] = send(
            part_relay.at[half], returned.at[2 * CAP : 3 * CAP, cols], return_sem, (half, 3), x_side[half]
        )

    def combine():
        for half in range(2):
            for name in ("high", "low", "far"):
                back_copies[name, half].wait_recv()

        def body(n):
            cols = columns(n, 256)
            token_out[:, cols] = dot_rows(place[...], returned[:, cols]).astype(bf16)
        loop(8, body)

    def add_into(ref, index, part):
        ref[index] = (wide(ref[index]) + wide(part)).astype(jnp.bfloat16)

    copies = {}

    def a_z(side, step, yy, received):
        off = (5 - step) if side == 0 else step - 5
        if received:
            copies["az", side, step - 1, yy].wait_recv()
            add_into(own_a, (zi(off), yy), az_buf[side, step - 2, yy])
        copies["az", side, step, yy] = send(
            own_a.at[zi(off), yy], az_buf.at[side, step - 1, yy], az_sem, (side, step - 1, yy),
            z_side[side],
        )

    def a_z_end(yy):
        total = wide(own_a[z, yy])
        for side in range(2):
            copies["az", side, 4, yy].wait_recv()
            total = total + wide(az_buf[side, 3, yy])
        own_a[z, yy] = total.astype(jnp.bfloat16)

    half_rows = {("ay", 0): slice(0, 32), ("ay", 1): slice(32, 48), ("bz", 0): slice(32, 48), ("bz", 1): slice(0, 32)}

    def a_y(side, step):
        off = (3 - step) if side == 0 else step - 3
        rows = half_rows["ay", side]
        if step == 1:
            copies["ay", side, 1] = send(
                own_a.at[z, yi(off), rows], ay_buf.at[side, 0, rows], ay_sem, (side, 0),
                y_side[side],
            )
            return
        copies["ay", side, 1].wait_recv()
        add_into(own_a, (z, yi(off), rows), ay_buf[side, 0, rows])
        copies["ay", side, 2] = send(
            own_a.at[z, yi(off)], ay_buf.at[side, 1], ay_sem, (side, 1),
            y_side[side],
        )

    def finish(total, lo):
        total = total * (1.0 / (CHIPS_Z * CHIPS_Y * CORES))
        width = total.shape[1]
        gate_out[:, lo : lo + width] = total[:32]
        down_out[:, lo : lo + width] = total[32:40]
        down_out[:, WIDTH + lo : WIDTH + lo + width] = total[40:48]

    def a_end():
        total = wide(own_a[z, y])
        for side in range(2):
            copies["ay", side, 2].wait_recv()
            total = total + wide(ay_buf[side, 1])
        finish(total, 0)

    def b_y(side, step, piece, received):
        off = (3 - step) if side == 0 else step - 3
        at_z = zi(piece)
        slot = ORDER_Z.index(piece)
        if received:
            copies["by", side, step - 1, piece].wait_recv()
            add_into(own_b, (yi(off), at_z), by_buf[side, step - 2, slot])
        copies["by", side, step, piece] = send(
            own_b.at[yi(off), at_z], by_buf.at[side, step - 1, slot], by_sem, (side, step - 1, slot),
            y_side[side],
        )

    def b_y_end(piece):
        total = wide(own_b[y, zi(piece)])
        for side in range(2):
            copies["by", side, 2, piece].wait_recv()
            total = total + wide(by_buf[side, 1, ORDER_Z.index(piece)])
        own_b[y, zi(piece)] = total.astype(jnp.bfloat16)

    def b_z(side, step):
        off = (5 - step) if side == 0 else step - 5
        rows = half_rows["bz", side] if step == 1 else slice(0, 48)
        if step > 1:
            before = half_rows["bz", side] if step == 2 else slice(0, 48)
            copies["bz", side, step - 1].wait_recv()
            add_into(own_b, (y, zi(off), before), bz_buf[side, step - 2, before])
        copies["bz", side, step] = send(
            own_b.at[y, zi(off), rows], bz_buf.at[side, step - 1, rows], bz_sem, (side, step - 1),
            z_side[side],
        )

    def b_end():
        total = wide(own_b[y, z])
        for side in range(2):
            copies["bz", side, 4].wait_recv()
            total = total + wide(bz_buf[side, 3])
        finish(total, COLS_A)

    upper, lower = (4, 3, 2, 1), (-3, -2, -1, 0)
    edge = {0: (0, 1), 1: (2, 3)}
    early_b = {0: upper, 1: lower}

    def pieces_a(step, fresh, received):
        for piece in range(2):
            for side in range(2):
                a_z(side, step, edge[1 - side if fresh else side][piece], received)

    def pieces_b(step, fresh, received, which):
        for piece in which:
            for side in range(2):
                b_y(side, step, early_b[1 - side if fresh else side][piece], received)

    def both_sides(action, step):
        for side in range(2):
            action(side, step)

    take_group_a(4)
    pieces_a(1, False, False)
    take_group_a(3)
    take_group_a(-3)
    pieces_a(2, True, False)
    take_group_b(2)
    pieces_b(1, False, False, range(4))
    take_group_b(1)
    take_group_b(-1)
    pieces_b(2, True, False, range(4))
    token_columns(0)
    token_columns(1)
    pieces_a(2, False, True)
    token_columns(2)
    token_columns(3)
    give_back(0)
    take_group_a(2)
    take_group_a(-2)
    pieces_a(3, True, True)
    pieces_b(2, False, True, range(2))
    token_columns(4)
    token_columns(5)
    take_group_a(1)
    take_group_a(-1)
    pieces_a(3, False, True)
    pieces_b(2, False, True, range(2, 4))
    token_columns(6)
    token_columns(7)
    give_back(1)
    take_group_b(0)
    take_group_a(0)
    pieces_a(4, True, True)
    b_y_end(4)
    both_sides(b_z, 1)
    pieces_a(4, False, True)
    pass_on(0)
    b_y_end(3)
    b_y_end(-3)
    both_sides(b_z, 2)
    b_y_end(2)
    b_y_end(-2)
    both_sides(b_z, 3)
    b_y_end(1)
    b_y_end(-1)
    b_y_end(0)
    pass_on(1)
    for yy in (2, 3, 0, 1):
        a_z_end(yy)
    both_sides(a_y, 1)
    both_sides(b_z, 4)
    both_sides(a_y, 2)
    combine()
    b_end()
    a_end()
    for copy in started:
        copy.wait_send()


ORDER_PAIR = (4, -3, 3, -2, 2, -1, 1, 0)


def on_device(
    tokens, cotangent, expert_ids, gate_probs, gate_up_weight, down_weight, down_residual
):
    bf16, f32 = jnp.bfloat16, jnp.float32
    sems = pltpu.SemaphoreType.DMA
    vmem, anywhere = pl.BlockSpec(memory_space=pltpu.VMEM), pl.BlockSpec(memory_space=pl.ANY)
    shapes = (
        ((TOK, MODEL), bf16), ((TOK, MODEL), bf16), ((MODEL, WIDTH), bf16), ((UNITS, MODEL), bf16),
        ((UNITS, MODEL), bf16), ((WIDTH, MODEL), bf16), ((MODEL, UNITS), bf16),
        ((ROWS, TOK), bf16), ((ROWS, TOK), f32), ((3 * CAP, MODEL), bf16), ((3 * CAP, MODEL), bf16),
        ((CAP, MODEL), bf16), ((CAP, MODEL), bf16),
        ((ROWS, MODEL), bf16), ((ROWS, MODEL), bf16), ((ROWS, WIDTH), f32), ((ROWS, WIDTH), bf16),
        ((ROWS, UNITS), bf16), ((MODEL, WIDTH), f32), ((UNITS, MODEL), f32),
        ((ROWS, MODEL), bf16), ((2, CAP, MODEL // 2), bf16), ((ROWS, MODEL), bf16),
        ((CORES, CHIPS_Z, CHIPS_Y, SHARE, COLS_A), bf16), ((CORES, CHIPS_Y, CHIPS_Z, SHARE, COLS_B), bf16),
        ((CHIPS_Z, CHIPS_Y, SHARE, COLS_A), bf16), ((CHIPS_Y, CHIPS_Z, SHARE, COLS_B), bf16),
        ((2, 4, CHIPS_Y, SHARE, COLS_A), bf16), ((2, 2, SHARE, COLS_A), bf16),
        ((2, 2, CHIPS_Z, SHARE, COLS_B), bf16), ((2, 4, SHARE, COLS_B), bf16),
    )
    semaphores = ((5,), (2, 8), (2, 2, 4), (2, 8), (2, 4), (2, 2, 4, 4), (2, 2, 2), (2, 2, 2, 8), (2, 2, 4))
    token_grad, gate_up_part, down_part = pl.pallas_call(
        layer_kernel,
        out_shape=(
            jax.ShapeDtypeStruct((TOK, MODEL), bf16),
            jax.ShapeDtypeStruct((GATE_ROWS, WIDTH), f32),
            jax.ShapeDtypeStruct((DOWN_ROWS, MODEL), f32),
        ),
        in_specs=[vmem, vmem, anywhere, anywhere, anywhere, anywhere, anywhere],
        out_specs=(vmem, vmem, vmem),
        scratch_shapes=[pltpu.VMEM(*shape) for shape in shapes] + [sems(shape) for shape in semaphores],
        compiler_params=pltpu.CompilerParams(
            collective_id=0, has_side_effects=True, vmem_limit_bytes=62 * 1024 * 1024
        ),
    )(
        expert_ids.T, gate_probs.T, tokens, cotangent, gate_up_weight[0], down_weight[0], down_residual[0, 0]
    )
    return (token_grad, gate_up_part[None], down_part[None])


def solution(mesh):
    placed = (
        P(("dp", "expert"), None),
        P(("dp", "expert"), None),
        P(("dp", "expert"), None),
        P(("dp", "expert"), None),
        P("expert", None, None),
        P("expert", None, None),
        P("dp", "expert", None, None),
    )
    return jax.shard_map(
        on_device,
        mesh=mesh,
        in_specs=placed,
        out_specs=(P(("dp", "expert"), None), P("expert", "dp", None), P("expert", "dp", None)),
        check_vma=False,
    )
```

time: 403 us -> 80.8 us (0.20); the launches traced: 398 us -> 80.5 us
  blocking collectives: 303 us -> 0 us
  Pallas kernels: 0 us -> 75 us
  matrix products: 18.8 us -> 0 us
  waiting for transfers between devices: 18.3 us -> 0 us
  other arithmetic: 15.2 us -> 0 us
  between operations: 14.9 us -> 0.64 us
  starting transfers between devices: 12.1 us -> 0 us
  local copies, waits for them, and re-layouts: 16.2 us -> 4.92 us
    unnamed x1 -> x0, blocking collectives: 303 us -> none
    pallas_call x0 -> x1, Pallas kernels: none -> 75 us  [on_device(): pl.pallas_call(layer_kernel, out_shape=(jax.ShapeDtypeStruct((TOK, MODEL)...]
    dot_general x5 -> x0, matrix products: 18.8 us -> none  [the longest x1 5.27 us: expert_forward(): projected = jnp.dot(token_rows, gate_up, preferred_element_type=jnp.float32)]
    all_to_all x3 -> x0, waiting for transfers between devices: 18.2 us -> none  [the longest x1 9.48 us: on_device(): lax.all_to_all(send_rows, 'expert', split_axis=0, concat_axis=0, tiled=True)]
    gather x9 -> x0, local copies, waits for them, and re-layouts: 13 us -> none  [the longest x2 4.17 us: on_device(): returned[pick_rows].astype(jnp.float32)]
    all_to_all x3 -> x0, starting transfers between devices: 12.1 us -> none  [the longest x1 4.97 us: on_device(): lax.all_to_all(send_rows, 'expert', split_axis=0, concat_axis=0, tiled=True)]
    convert_element_type x2 -> x0, other arithmetic: 6.94 us -> none  [the longest x1 4.26 us: on_device(): gate_up_wide = lax.optimization_barrier(gate_up_round).astype(jnp.float32)]
  transfers between devices with their start and end apart: 4 -> 0, of which waited for: 2 -> 0; matrix products, arithmetic and copies ran while one was open for 8% -> 0% of each run, Pallas kernels for 0% -> 0%
where the time goes in v2:
time: 80.8 us; the launch traced here: 80.5 us
  Pallas kernels  75 us (93%)
  local copies, waits for them, and re-layouts  4.92 us (6%)
    pallas_call x1, Pallas kernels, on_device(): pl.pallas_call(layer_kernel, out_shape=(jax.ShapeDtypeStruct((TOK, MODEL)...  75 us
    unnamed x3, local copies, waits for them, and re-layouts  4.92 us

profile of v2, /device:TPU:1, one launch (start us, length us, event | category | flops | bytes accessed | tf_op | source)
XLA Modules:
  0.0 80.5 jit_solution(7793393858240646169)
XLA Ops:
  0.6 75.0 %shard_map.94 = (bf16[128,2048]{1,0:T(8,128)(2,1)}, f32[32,1024]{1,0:T(8,128)}, f32[8,2048]{1,0:T(8,128)}) custom-call(s32[2,128]{1,0:T(2,128)} %bitcast.12, f32[2,128]{1,0:T(2,128)} %bitcast.13, bf16[128,2048]{1,0:T(8,128)(2,1)} %tokens_hbm.1, bf16[128,2048]{1,0:T(8,128)(2,1)} %cotangent_hbm.1, bf16[2048,1024]{1,0:T(8,128)(2,1)} %bitcast.7, ...), custom_call_target="tpu_custom_call" | custom-call | tf_op jit(solution)/shard_map/pallas_call | solution.py:517
  75.6 1.9 %copy.13 = bf16[128,2048]{1,0:T(8,128)(2,1)} copy(bf16[128,2048]{1,0:T(8,128)(2,1)} %get-tuple-element.12) | data formatting | bytes 1048576
  77.5 1.6 %copy.14 = f32[1,32,1024]{2,1,0:T(8,128)} copy(f32[1,32,1024]{2,1,0:T(8,128)} %bitcast.10) | data formatting | bytes 262144
  79.1 1.5 %copy.15 = f32[1,8,2048]{2,1,0:T(8,128)} copy(f32[1,8,2048]{2,1,0:T(8,128)} %bitcast.11) | data formatting | bytes 131072

commit v3 on v2

v3 whole, which is shorter than its diff:
```python
import jax
import jax.numpy as jnp
from jax import lax
from jax.experimental import pallas as pl
from jax.experimental.pallas import tpu as pltpu
from jax.sharding import PartitionSpec as P

MESH = pl.DeviceIdType.MESH
CHIPS_Z, CHIPS_Y, CORES, EXPERTS = 8, 4, 2, 4
SHARE, WIDTH, HALF = 96, 1024, 512
GATE_ROWS, DOWN_ROWS = 32, 8
ROWS_A = 48
ROWS_B = SHARE - ROWS_A
FAR_PARTS = ((0, 32), (32, ROWS_B))
GROUPS = (4, -3, 3, -2, 2, -1, 1, 0)
ORDER_Y = (2, 1, -1, 0)
TOK, CAP, MODEL, UNITS = 128, 80, 2048, 512
ROWS = EXPERTS * CAP
OPP, SELF, LOW, HIGH = (slice(k * CAP, (k + 1) * CAP) for k in range(4))
EARLY, LATE, NEAR = slice(0, 2 * CAP), slice(2 * CAP, ROWS), slice(CAP, ROWS)


def wide(value):
    return value.astype(jnp.float32)


def dot(left, right):
    return jnp.dot(left, right, preferred_element_type=jnp.float32)


def dot_rows(left, right):
    return lax.dot_general(left, right, (((0,), (0,)), ((), ())), preferred_element_type=jnp.float32)


def columns(index, width):
    return pl.ds(pl.multiple_of(index * width, width), width)


def loop(count, body):
    def step(index, carry):
        body(index)
        return carry

    lax.fori_loop(0, count, step, 0)


def layer_kernel(
    ids_hbm, probs_hbm, tokens_hbm, cotangent_hbm, gate_up_hbm, down_hbm, residual_hbm,
    token_out, gate_out, down_out,
    ids_ref, probs_ref, tok_in, cot_in, gate_up, down, residual, gate_up_t, down_t,
    place, slot_weight, tok_send, grad_send, tok_relay, grad_relay,
    tok_all, grad_all, both, back, hidden, sum_gate, sum_down,
    tok_early, tok_late, hid_early, hid_late, tok_early_pair, tok_late_pair, hid_early_pair, hid_late_pair,
    grad_pair, back_pair, residual_pair,
    part, part_relay, returned,
    half_back, own, az_buf, ay_buf, by_buf, hub_buf, bz_buf, final, final_gate, final_down,
    load_sem, swap_sem, return_sem, pair_sem, az_sem, ay_sem, by_sem, hub_sem, bz_sem,
):
    bf16 = jnp.bfloat16
    me, x = lax.axis_index("dp"), lax.axis_index("expert")
    z, y, core = me // (CHIPS_Y * CORES), (me // CORES) % CHIPS_Y, me % CORES

    def at(zz, yy, cc):
        return (((zz + CHIPS_Z) % CHIPS_Z) * CHIPS_Y + (yy + CHIPS_Y) % CHIPS_Y) * CORES + cc

    def zi(off):
        return (z + off + CHIPS_Z) % CHIPS_Z

    def yi(off):
        return (y + off + CHIPS_Y) % CHIPS_Y

    partner = (at(z, y, 1 - core), x)
    z_side = ((at(z + 1, y, core), x), (at(z - 1, y, core), x))
    y_side = ((at(z, y + 1, core), x), (at(z, y - 1, core), x))
    x_side = ((me, (x + 1) % EXPERTS), (me, (x + EXPERTS - 1) % EXPERTS))
    barrier = pltpu.get_barrier_semaphore()
    z_far = [(at(z + off, y, core), x) for off in (2, -2)]
    y_far = [(at(z, y + 2, core), x)]
    for device in (partner, *z_side, *y_side, *x_side, *z_far, *y_far):
        pl.semaphore_signal(barrier, inc=1, device_id=device, device_id_type=MESH)

    loads = [
        pltpu.make_async_copy(source, target, load_sem.at[k])
        for k, (source, target) in enumerate(
            (
                (ids_hbm, ids_ref),
                (probs_hbm, probs_ref),
                (tokens_hbm, tok_in),
                (cotangent_hbm, cot_in),
                (down_hbm, down),
                (gate_up_hbm, gate_up),
                (residual_hbm, residual),
            )
        )
    ]
    for copy in loads:
        copy.start()

    started = []

    def send(src, dst, sems, index, device):
        copy = pltpu.make_async_remote_copy(
            src_ref=src, dst_ref=dst, send_sem=sems.at[(0, *index)], recv_sem=sems.at[(1, *index)],
            device_id=device, device_id_type=MESH,
        )
        copy.start()
        started.append(copy)
        return copy

    loads[0].wait()
    loads[1].wait()
    ids, probs = ids_ref[...], probs_ref[...]
    before = lax.broadcasted_iota(jnp.int32, (TOK, TOK), 0) < lax.broadcasted_iota(jnp.int32, (TOK, TOK), 1)
    before = jnp.where(before, 1.0, 0.0).astype(bf16)
    slots = wide(lax.broadcasted_iota(jnp.int32, (CAP, TOK), 0))
    for k in range(EXPERTS):
        expert = (x + k) % EXPERTS
        hits = ids == expert
        member = jnp.sum(jnp.where(hits, 1.0, 0.0), axis=0, keepdims=True)
        weight = jnp.sum(jnp.where(hits, probs, 0.0), axis=0, keepdims=True)
        index = dot(jnp.broadcast_to(member, (8, TOK)).astype(bf16), before)[0:1]
        chosen = jnp.where((slots == index) & (member > 0.5), 1.0, 0.0)
        rows = slice(k * CAP, (k + 1) * CAP)
        place[rows] = chosen.astype(bf16)
        slot_weight[rows] = jnp.broadcast_to(jnp.sum(chosen * weight, axis=1, keepdims=True), (CAP, TOK))

    def pick_tokens(k, target, rows):
        def body(n):
            cols = columns(n, 512)
            target[rows, cols] = dot(place[k * CAP : (k + 1) * CAP], tok_in[:, cols]).astype(bf16)
        loop(4, body)

    def pick_grads(k, target, rows):
        def body(n):
            cols = columns(n, 512)
            block = slice(k * CAP, (k + 1) * CAP)
            value = dot(place[block], cot_in[:, cols]) * slot_weight[block, 0:1]
            target[rows, cols] = value.astype(bf16)
        loop(4, body)

    swap = {}
    first, second, third = slice(0, CAP), slice(CAP, 2 * CAP), slice(2 * CAP, 3 * CAP)
    loads[2].wait()
    pick_tokens(2, tok_send, second)
    pl.semaphore_wait(barrier, 10)
    swap["tok", "leg"] = send(tok_send.at[second], tok_relay, swap_sem, (0,), x_side[0])
    loads[3].wait()
    pick_grads(2, grad_send, second)
    swap["grad", "leg"] = send(grad_send.at[second], grad_relay, swap_sem, (1,), x_side[1])
    pick_tokens(1, tok_send, first)
    left, right = slice(0, 1024), slice(1024, 2048)
    swap["tok", 0, 0] = send(tok_send.at[first, left], tok_all.at[LOW, left], swap_sem, (2,), x_side[0])
    pick_tokens(3, tok_send, third)
    swap["tok", 1, 0] = send(tok_send.at[third, left], tok_all.at[HIGH, left], swap_sem, (3,), x_side[1])
    pick_grads(1, grad_send, first)
    pick_grads(3, grad_send, third)
    pick_tokens(0, tok_all, SELF)
    pick_grads(0, grad_all, SELF)
    loads[4].wait()

    def turn_down(n):
        rows = columns(n, 256)
        down_t[rows, :] = down[:, rows].T

    loop(8, turn_down)
    swap["tok", "leg"].wait_recv()
    swap["tok", "far"] = send(tok_relay, tok_all.at[OPP], swap_sem, (4,), x_side[0])
    swap["grad", "leg"].wait_recv()
    swap["grad", "far"] = send(grad_relay, grad_all.at[OPP], swap_sem, (5,), x_side[1])
    swap["tok", 0, 1] = send(tok_send.at[first, right], tok_all.at[LOW, right], swap_sem, (10,), x_side[0])
    swap["tok", 1, 1] = send(tok_send.at[third, right], tok_all.at[HIGH, right], swap_sem, (11,), x_side[1])
    mine, theirs = columns(core, WIDTH), columns(1 - core, WIDTH)
    for part_at, cols in enumerate((theirs, mine)):
        swap["grad", 0, part_at] = send(
            grad_send.at[first, cols], grad_all.at[LOW, cols], swap_sem, (6 + part_at,), x_side[0]
        )
        swap["grad", 1, part_at] = send(
            grad_send.at[third, cols], grad_all.at[HIGH, cols], swap_sem, (8 + part_at,), x_side[1]
        )
    pair = {}

    def to_partner(name, index, src, dst):
        pair[name] = send(src, dst, pair_sem, (index,), partner)

    to_partner("grad self", 1, grad_all.at[SELF, theirs], grad_pair.at[SELF])
    loads[5].wait()

    def turn_gate_up(n):
        rows = columns(n, 256)
        gate_up_t[:, rows] = gate_up[rows, :].T

    loop(8, turn_gate_up)
    loads[6].wait()

    def project(rows):
        def body(n):
            cols = columns(n, 256)
            both[rows, cols] = dot(tok_all[rows], gate_up[:, cols])
        loop(4, body)

        def gates(n):
            r = pl.ds(pl.multiple_of(rows.start + n * 16, 16), 16)
            gate, up = both[r, 0:UNITS], both[r, UNITS : 2 * UNITS]
            sig = jax.nn.sigmoid(gate)
            active = gate * sig
            hidden[r] = (active * up).astype(bf16)
            both[r, 0:UNITS] = up * sig * (1.0 + gate * (1.0 - sig))
            both[r, UNITS : 2 * UNITS] = active
        loop((rows.stop - rows.start) // 16, gates)

    def pull_back(rows):
        def body(n):
            cols, upper = columns(n, 256), columns(n + 2, 256)
            value = dot(grad_all[rows], down_t[:, cols])
            back[rows, cols] = (value * both[rows, cols]).astype(bf16)
            back[rows, upper] = (value * both[rows, upper]).astype(bf16)
        loop(2, body)

    my_units, their_units = columns(core, HALF), columns(1 - core, HALF)
    to_partner("residual", 2, residual.at[:, theirs], residual_pair)
    def turn_tokens(rows, target):
        def body(n):
            cols = columns(n, 256)
            target[cols, :] = tok_all[rows, cols].T
        loop(8, body)

    def turn_hidden(rows, target):
        def body(n):
            cols = columns(n, 256)
            target[cols, :] = hidden[rows, cols].T
        loop(2, body)

    project(SELF)
    swap["tok", "far"].wait_recv()
    turn_tokens(EARLY, tok_early)
    to_partner("tok early", 4, tok_early, tok_early_pair)
    swap["grad", "far"].wait_recv()
    to_partner("grad far", 6, grad_all.at[OPP, theirs], grad_pair.at[OPP])
    project(OPP)
    turn_hidden(EARLY, hid_early)
    to_partner("hidden early", 5, hid_early, hid_early_pair)
    pull_back(EARLY)
    to_partner("back early", 7, back.at[EARLY, their_units], back_pair.at[EARLY])

    def down_columns(half):
        return pl.ds(pl.multiple_of(core * WIDTH + half * 512, 512), 512)

    for name in ("residual", "grad self", "grad far", "hidden early"):
        pair[name].wait_recv()

    def early_down(n):
        rows = columns(n, 128)
        for half in range(2):
            cols = slice(half * 512, half * 512 + 512)
            start = wide(residual[rows, down_columns(half)]) + wide(residual_pair[rows, cols])
            start = start + dot(hid_early[rows], grad_all[EARLY, down_columns(half)])
            sum_down[rows, cols] = start + dot(hid_early_pair[rows], grad_pair[EARLY, cols])
    loop(4, early_down)
    for name in ("tok early", "back early"):
        pair[name].wait_recv()

    def early_gate(n):
        rows = columns(n, 256)
        value = dot(tok_early[rows], back[EARLY, my_units])
        sum_gate[rows, :] = value + dot(tok_early_pair[rows], back_pair[EARLY])
    loop(8, early_gate)

    for part_at in range(2):
        for side in range(2):
            swap["tok", side, part_at].wait_recv()
    turn_tokens(LATE, tok_late)
    to_partner("tok late", 0, tok_late, tok_late_pair)
    project(LATE)
    turn_hidden(LATE, hid_late)
    to_partner("hidden late", 3, hid_late, hid_late_pair)
    swap["grad", 0, 0].wait_recv()
    to_partner("grad low", 9, grad_all.at[LOW, theirs], grad_pair.at[LOW])
    swap["grad", 1, 0].wait_recv()
    to_partner("grad high", 10, grad_all.at[HIGH, theirs], grad_pair.at[HIGH])

    def half_pull(n):
        cols = columns(n, 256)
        half_back[:, cols] = dot(grad_all[LATE, theirs], down_t[theirs, cols])
    loop(2, half_pull)
    swap["grad", 0, 1].wait_recv()
    swap["grad", 1, 1].wait_recv()

    def late_pull(n):
        cols, upper = columns(n, 256), columns(n + 2, 256)
        value = half_back[:, cols] + dot(grad_all[LATE, mine], down_t[mine, cols])
        back[LATE, cols] = (value * both[LATE, cols]).astype(bf16)
        back[LATE, upper] = (value * both[LATE, upper]).astype(bf16)
    loop(2, late_pull)
    to_partner("back late", 11, back.at[LATE, their_units], back_pair.at[LATE])
    def late_gate(n):
        rows = columns(n, 256)
        sum_gate[rows, :] += dot(tok_late[rows], back[LATE, my_units])
    loop(8, late_gate)
    for name in ("grad low", "grad high", "hidden late"):
        pair[name].wait_recv()

    def late_down(n):
        rows = columns(n, 128)
        for half in range(2):
            cols = slice(half * 512, half * 512 + 512)
            value = dot(hid_late[rows], grad_all[LATE, down_columns(half)])
            sum_down[rows, cols] += value + dot(hid_late_pair[rows], grad_pair[LATE, cols])
    loop(4, late_down)
    for name in ("tok late", "back late"):
        pair[name].wait_recv()

    def group(off):
        zz = zi(off)
        rows = columns(zz, 256)
        value = sum_gate[rows, :] + dot(tok_late_pair[rows], back_pair[LATE])
        for yy in range(CHIPS_Y):
            down_rows = pl.ds(pl.multiple_of(zz * 64 + yy * 16, 16), 16)
            own[zz, yy, 0:64] = value[64 * yy : 64 * yy + 64].astype(bf16)
            own[zz, yy, 64:80] = sum_down[down_rows, 0:512].astype(bf16)
            own[zz, yy, 80:96] = sum_down[down_rows, 512:1024].astype(bf16)

    back_copies = {}

    def token_columns(n):
        cols = slice(n * 256, n * 256 + 256)
        value = dot(back[...], gate_up_t[:, cols]).astype(bf16)
        part[:, cols] = value
        returned[0:CAP, cols] = value[SELF]

    def give_back(half):
        cols = slice(half * 1024, half * 1024 + 1024)
        other = x_side[half]
        back_copies["high", half] = send(
            part.at[HIGH, cols], returned.at[3 * CAP : 4 * CAP, cols], return_sem, (half, 0), x_side[0]
        )
        back_copies["low", half] = send(
            part.at[LOW, cols], returned.at[CAP : 2 * CAP, cols], return_sem, (half, 1), x_side[1]
        )
        back_copies["leg", half] = send(
            part.at[OPP, cols], part_relay.at[half], return_sem, (half, 2), other
        )

    def pass_on(half):
        cols = slice(half * 1024, half * 1024 + 1024)
        back_copies["leg", half].wait_recv()
        back_copies["far", half] = send(
            part_relay.at[half], returned.at[2 * CAP : 3 * CAP, cols], return_sem, (half, 3), x_side[half]
        )

    def combine():
        for half in range(2):
            for name in ("high", "low", "far"):
                back_copies[name, half].wait_recv()

        def body(n):
            cols = columns(n, 256)
            token_out[:, cols] = dot_rows(place[...], returned[:, cols]).astype(bf16)
        loop(8, body)

    rows_a, rows_b = slice(0, ROWS_A), slice(ROWS_A, SHARE)
    copies = {}

    def add_into(zz, yy, rows, arrived):
        own[zz, yy, rows] = (wide(own[zz, yy, rows]) + wide(arrived)).astype(bf16)

    def a_z(side, step, off_y):
        off = (5 - step) if side == 0 else step - 5
        slot = ORDER_Y.index(off_y)
        if ("az", side, step - 1, off_y) in copies:
            copies["az", side, step - 1, off_y].wait_recv()
            add_into(zi(off), yi(off_y), rows_a, az_buf[side, step - 2, slot])
        copies["az", side, step, off_y] = send(
            own.at[zi(off), yi(off_y), rows_a], az_buf.at[side, step - 1, slot], az_sem,
            (side, step - 1, slot), z_side[side],
        )

    def a_z_end(off_y):
        slot = ORDER_Y.index(off_y)
        total = wide(own[z, yi(off_y), rows_a])
        for side in range(2):
            copies["az", side, 4, off_y].wait_recv()
            total = total + wide(az_buf[side, 3, slot])
        if off_y == 0:
            return total
        own[z, yi(off_y), rows_a] = total.astype(bf16)
        copies["ay", off_y] = send(
            own.at[z, yi(off_y), rows_a], ay_buf.at[slot], ay_sem, (slot,), (at(z, y + off_y, core), x)
        )

    def finish(total, rows):
        final[rows] = total * (1.0 / (CHIPS_Z * CHIPS_Y * CORES))

    def a_end(total):
        for off_y in (2, 1, -1):
            copies["ay", off_y].wait_recv()
            total = total + wide(ay_buf[ORDER_Y.index(off_y)])
        finish(total, rows_a)

    def b_y(side, step, piece):
        off = (3 - step) if side == 0 else step - 3
        slot = GROUPS.index(piece)
        if ("by", side, step - 1, piece) in copies:
            copies["by", side, step - 1, piece].wait_recv()
            add_into(zi(piece), yi(off), rows_b, by_buf[side, step - 2, slot])
        copies["by", side, step, piece] = send(
            own.at[zi(piece), yi(off), rows_b], by_buf.at[side, step - 1, slot], by_sem,
            (side, step - 1, slot), y_side[side],
        )

    def b_y_end(piece):
        slot = GROUPS.index(piece)
        total = wide(own[zi(piece), y, rows_b])
        for side in range(2):
            copies["by", side, 2, piece].wait_recv()
            total = total + wide(by_buf[side, 1, slot])
        if piece == 0:
            return total
        src = own.at[zi(piece), y]
        src[rows_b] = total.astype(bf16)
        if piece == 4:
            for side, (lo, hi) in enumerate(FAR_PARTS):
                copies["far", side] = send(
                    src.at[ROWS_A + lo : ROWS_A + hi], hub_buf.at[side, 0, lo:hi], hub_sem, (side, 0),
                    (at(z + (2, -2)[side], y, core), x),
                )
        elif abs(piece) == 3:
            side = 0 if piece > 0 else 1
            copies["near", side] = send(src.at[rows_b], hub_buf.at[side, 1], hub_sem, (side, 1), z_side[side])
        elif abs(piece) == 2:
            side = 0 if piece > 0 else 1
            lo, hi = FAR_PARTS[side]
            copies["far", side].wait_recv()
            copies["near", side].wait_recv()
            part_rows = slice(ROWS_A + lo, ROWS_A + hi)
            src[rows_b] = (wide(src[rows_b]) + wide(hub_buf[side, 1])).astype(bf16)
            src[part_rows] = (wide(src[part_rows]) + wide(hub_buf[side, 0, lo:hi])).astype(bf16)
            copies["bz", piece] = send(
                src.at[rows_b], bz_buf.at[side], bz_sem, (side,), (at(z + piece, y, core), x)
            )
        else:
            side = 0 if piece > 0 else 1
            copies["bz", piece] = send(src.at[rows_b], bz_buf.at[2 + side], bz_sem, (2 + side,), z_side[side])

    def b_end(total):
        for slot, piece in enumerate((2, -2, 1, -1)):
            copies["bz", piece].wait_recv()
            total = total + wide(bz_buf[slot])
        finish(total, rows_b)

    def final_swap():
        other = 1 - core
        gate_rows = pl.ds(pl.multiple_of(32 * other, 32), 32)
        last = [send(final.at[gate_rows], final_gate, bz_sem, (4,), partner)]
        for k in range(2):
            down_rows = pl.ds(pl.multiple_of(64 + 16 * k + 8 * other, 8), 8)
            last.append(send(final.at[down_rows], final_down.at[k], bz_sem, (5 + k,), partner))
        gate_out[:, my_units] = final[pl.ds(pl.multiple_of(32 * core, 32), 32)]
        for k in range(2):
            down_out[:, down_columns(k)] = final[pl.ds(pl.multiple_of(64 + 16 * k + 8 * core, 8), 8)]
        for copy in last:
            copy.wait_recv()
        gate_out[:, their_units] = final_gate[...]
        for k in range(2):
            cols = pl.ds(pl.multiple_of(other * WIDTH + k * 512, 512), 512)
            down_out[:, cols] = final_down[k]

    upper = (4, 3, 2, 1)
    edge = {0: (2, 1), 1: (-1, 0)}

    def b_start(piece):
        far = 0 if piece in upper else 1
        b_y(far, 1, piece)
        b_y(1 - far, 2, piece)

    def b_next(piece):
        b_y(0 if piece in upper else 1, 2, piece)

    def a_step(step, own_edge):
        for k in range(2):
            for side in range(2):
                a_z(side, step, edge[side if own_edge else 1 - side][k])

    group(4)
    a_step(1, True)
    b_start(4)
    group(-3)
    for off_y in edge[0]:
        a_z(1, 2, off_y)
    group(3)
    for off_y in edge[1]:
        a_z(0, 2, off_y)
    b_start(-3)
    b_start(3)
    for off in GROUPS[3:]:
        group(off)
        if off in (-2, 2):
            b_start(off)
    for n in range(4):
        token_columns(n)
    give_back(0)
    a_step(2, True)
    b_start(-1)
    token_columns(4)
    b_next(4)
    b_start(1)
    a_step(3, False)
    b_next(-3)
    token_columns(5)
    b_next(3)
    b_start(0)
    token_columns(6)
    a_step(3, True)
    b_next(-2)
    b_y_end(4)
    token_columns(7)
    give_back(1)
    b_next(2)
    b_y_end(-3)
    a_step(4, False)
    b_y_end(3)
    b_next(-1)
    b_next(1)
    b_y_end(-2)
    a_step(4, True)
    b_next(0)
    b_y_end(2)
    pass_on(0)
    b_y_end(-1)
    a_z_end(2)
    a_z_end(-1)
    b_y_end(1)
    a_z_end(1)
    total_b = b_y_end(0)
    total_a = a_z_end(0)
    pass_on(1)
    final[rows_a], final[rows_b] = total_a, total_b
    combine()
    a_end(final[rows_a])
    b_end(final[rows_b])
    final_swap()
    for copy in started:
        copy.wait_send()


def store_kernel(*refs):
    sources, targets, sems = refs[:3], refs[3:6], refs[6]
    stores = [pltpu.make_async_copy(sources[k], targets[k], sems.at[k]) for k in range(3)]
    for copy in stores:
        copy.start()
    for copy in stores:
        copy.wait()


def on_device(
    tokens, cotangent, expert_ids, gate_probs, gate_up_weight, down_weight, down_residual
):
    bf16, f32 = jnp.bfloat16, jnp.float32
    sems = pltpu.SemaphoreType.DMA
    vmem, anywhere = pl.BlockSpec(memory_space=pltpu.VMEM), pl.BlockSpec(memory_space=pl.ANY)
    shapes = (
        ((2, TOK), jnp.int32), ((2, TOK), f32),
        ((TOK, MODEL), bf16), ((TOK, MODEL), bf16), ((MODEL, WIDTH), bf16), ((UNITS, MODEL), bf16),
        ((UNITS, MODEL), bf16), ((WIDTH, MODEL), bf16), ((MODEL, UNITS), bf16),
        ((ROWS, TOK), bf16), ((ROWS, TOK), f32), ((3 * CAP, MODEL), bf16), ((3 * CAP, MODEL), bf16),
        ((CAP, MODEL), bf16), ((CAP, MODEL), bf16),
        ((ROWS, MODEL), bf16), ((ROWS, MODEL), bf16), ((ROWS, WIDTH), f32), ((ROWS, WIDTH), bf16),
        ((ROWS, UNITS), bf16), ((MODEL, HALF), f32), ((UNITS, WIDTH), f32),
        *(2 * (((MODEL, 2 * CAP), bf16), ((MODEL, 2 * CAP), bf16), ((UNITS, 2 * CAP), bf16), ((UNITS, 2 * CAP), bf16))),
        ((ROWS, WIDTH), bf16), ((ROWS, HALF), bf16), ((UNITS, WIDTH), bf16),
        ((ROWS, MODEL), bf16), ((2, CAP, MODEL // 2), bf16), ((ROWS, MODEL), bf16),
        ((2 * CAP, UNITS), f32), ((CHIPS_Z, CHIPS_Y, SHARE, HALF), bf16),
        ((2, 4, CHIPS_Y, ROWS_A, HALF), bf16), ((3, ROWS_A, HALF), bf16),
        ((2, 2, CHIPS_Z, ROWS_B, HALF), bf16), ((2, 2, ROWS_B, HALF), bf16), ((4, ROWS_B, HALF), bf16),
        ((SHARE, HALF), f32), ((GATE_ROWS, HALF), f32), ((2, DOWN_ROWS, HALF), f32),
    )
    semaphores = ((7,), (2, 12), (2, 2, 4), (2, 12), (2, 2, 4, 4), (2, 3), (2, 2, 2, 8), (2, 2, 2), (2, 7))
    results = (
        jax.ShapeDtypeStruct((TOK, MODEL), bf16),
        jax.ShapeDtypeStruct((GATE_ROWS, WIDTH), f32),
        jax.ShapeDtypeStruct((DOWN_ROWS, MODEL), f32),
    )
    values = pl.pallas_call(
        layer_kernel,
        out_shape=results,
        in_specs=[pl.BlockSpec(memory_space=pltpu.HBM)] * 7,
        out_specs=(vmem, vmem, vmem),
        scratch_shapes=[pltpu.VMEM(*shape) for shape in shapes] + [sems(shape) for shape in semaphores],
        compiler_params=pltpu.CompilerParams(
            collective_id=0, has_side_effects=True, vmem_limit_bytes=53 * 1024 * 1024
        ),
    )(
        expert_ids.T, gate_probs.T, tokens, cotangent, gate_up_weight[0], down_weight[0], down_residual[0, 0]
    )
    token_grad, gate_up_part, down_part = pl.pallas_call(
        store_kernel,
        out_shape=results,
        in_specs=[anywhere] * 3,
        out_specs=(anywhere,) * 3,
        scratch_shapes=[sems((3,))],
        compiler_params=pltpu.CompilerParams(vmem_limit_bytes=1024 * 1024),
    )(*values)
    return (token_grad, gate_up_part[None], down_part[None])


def solution(mesh):
    placed = (
        P(("dp", "expert"), None),
        P(("dp", "expert"), None),
        P(("dp", "expert"), None),
        P(("dp", "expert"), None),
        P("expert", None, None),
        P("expert", None, None),
        P("dp", "expert", None, None),
    )
    return jax.shard_map(
        on_device,
        mesh=mesh,
        in_specs=placed,
        out_specs=(P(("dp", "expert"), None), P("expert", "dp", None), P("expert", "dp", None)),
        check_vma=False,
    )
```

time: 80.8 us -> 77.2 us (0.955)
  local copies, waits for them, and re-layouts: 4.92 us -> 1.35 us
    unnamed x3 -> x4, local copies, waits for them, and re-layouts: 4.92 us -> 1.35 us
    pallas_call x1 -> x2, Pallas kernels: 75 us -> 75.1 us  [the longest x1 74.2 us: on_device(): pl.pallas_call(layer_kernel, out_shape=results, in_specs=[pl.BlockSpec(me...]
where the time goes in v3:
time: 77.2 us; the launch traced here: 77.1 us
  Pallas kernels  75.1 us (97%)
  local copies, waits for them, and re-layouts  1.35 us (2%)
    pallas_call x1, Pallas kernels, on_device(): pl.pallas_call(layer_kernel, out_shape=results, in_specs=[pl.BlockSpec(me...  74.2 us

profile of v3, /device:TPU:1, one launch (start us, length us, event | category | flops | bytes accessed | tf_op | source)
XLA Modules:
  0.0 77.1 jit_solution(8059605748589243373)
XLA Ops:
  0.6 0.0 copy-start
  0.6 0.7 copy-done
  1.3 0.0 copy-start.1
  1.3 0.7 copy-done.1
  2.0 74.2 %shard_map.94 = (bf16[128,2048]{1,0:T(8,128)(2,1)S(1)}, f32[32,1024]{1,0:T(8,128)S(1)}, f32[8,2048]{1,0:T(8,128)S(1)}) custom-call(s32[2,128]{1,0:T(2,128)S(1)} %bitcast.7, f32[2,128]{1,0:T(2,128)S(1)} %bitcast.8, bf16[128,2048]{1,0:T(8,128)(2,1)} %tokens_hbm.1, bf16[128,2048]{1,0:T(8,128)(2,1)} %cotangent_hbm.1, bf16[2048,1024]{1,0:T(8,128)(2,1)} %bitcast.9, ...), custom_call_target="tpu_custom_call" | custom-call | tf_op jit(solution)/shard_map/pallas_call | solution.py:582
  76.2 0.9 %shard_map.95 = (bf16[128,2048]{1,0:T(8,128)(2,1)}, f32[32,1024]{1,0:T(8,128)}, f32[8,2048]{1,0:T(8,128)}) custom-call(bf16[128,2048]{1,0:T(8,128)(2,1)S(1)} %get-tuple-element.9.refs_0_, f32[32,1024]{1,0:T(8,128)S(1)} %get-tuple-element.10.refs_1_, f32[8,2048]{1,0:T(8,128)S(1)} %get-tuple-element.11.refs_2_), custom_call_target="tpu_custom_call" | custom-call | tf_op jit(solution)/shard_map/pallas_call | solution.py:594
Async XLA Ops:
  0.6 0.7 copy-start
  1.3 0.7 copy-start.1

commit v4 on v3

--- a/solution.py
+++ b/solution.py
@@ -48,12 +48,12 @@
     ids_hbm, probs_hbm, tokens_hbm, cotangent_hbm, gate_up_hbm, down_hbm, residual_hbm,
     token_out, gate_out, down_out,
     ids_ref, probs_ref, tok_in, cot_in, gate_up, down, residual, gate_up_t, down_t,
-    place, slot_weight, tok_send, grad_send, tok_relay, grad_relay,
+    place, place_t, slot_weight, tok_send, grad_send, tok_relay, grad_relay,
     tok_all, grad_all, both, back, hidden, sum_gate, sum_down,
     tok_early, tok_late, hid_early, hid_late, tok_early_pair, tok_late_pair, hid_early_pair, hid_late_pair,
     grad_pair, back_pair, residual_pair,
     part, part_relay, returned,
-    half_back, own, az_buf, ay_buf, by_buf, hub_buf, bz_buf, final, final_gate, final_down,
+    half_back, own, az_buf, ay_buf, by_buf, hub_buf, bz_buf, final, final_pair,
     load_sem, swap_sem, return_sem, pair_sem, az_sem, ay_sem, by_sem, hub_sem, bz_sem,
 ):
     bf16 = jnp.bfloat16
@@ -190,6 +190,7 @@
         gate_up_t[:, rows] = gate_up[rows, :].T
 
     loop(8, turn_gate_up)
+    place_t[...] = place[...].T
     loads[6].wait()
 
     def project(rows):
@@ -242,6 +243,14 @@
     pull_back(EARLY)
     to_partner("back early", 7, back.at[EARLY, their_units], back_pair.at[EARLY])
 
+    for part_at in range(2):
+        for side in range(2):
+            swap["tok", side, part_at].wait_recv()
+    turn_tokens(LATE, tok_late)
+    to_partner("tok late", 0, tok_late, tok_late_pair)
+    project(LATE)
+    turn_hidden(LATE, hid_late)
+    to_partner("hidden late", 3, hid_late, hid_late_pair)
     def down_columns(half):
         return pl.ds(pl.multiple_of(core * WIDTH + half * 512, 512), 512)
 
@@ -265,14 +274,6 @@
         sum_gate[rows, :] = value + dot(tok_early_pair[rows], back_pair[EARLY])
     loop(8, early_gate)
 
-    for part_at in range(2):
-        for side in range(2):
-            swap["tok", side, part_at].wait_recv()
-    turn_tokens(LATE, tok_late)
-    to_partner("tok late", 0, tok_late, tok_late_pair)
-    project(LATE)
-    turn_hidden(LATE, hid_late)
-    to_partner("hidden late", 3, hid_late, hid_late_pair)
     swap["grad", 0, 0].wait_recv()
     to_partner("grad low", 9, grad_all.at[LOW, theirs], grad_pair.at[LOW])
     swap["grad", 1, 0].wait_recv()
@@ -330,14 +331,14 @@
     def give_back(half):
         cols = slice(half * 1024, half * 1024 + 1024)
         other = x_side[half]
+        back_copies["leg", half] = send(
+            part.at[OPP, cols], part_relay.at[half], return_sem, (half, 2), other
+        )
         back_copies["high", half] = send(
             part.at[HIGH, cols], returned.at[3 * CAP : 4 * CAP, cols], return_sem, (half, 0), x_side[0]
         )
         back_copies["low", half] = send(
             part.at[LOW, cols], returned.at[CAP : 2 * CAP, cols], return_sem, (half, 1), x_side[1]
-        )
-        back_copies["leg", half] = send(
-            part.at[OPP, cols], part_relay.at[half], return_sem, (half, 2), other
         )
 
     def pass_on(half):
@@ -347,15 +348,14 @@
             part_relay.at[half], returned.at[2 * CAP : 3 * CAP, cols], return_sem, (half, 3), x_side[half]
         )
 
-    def combine():
-        for half in range(2):
-            for name in ("high", "low", "far"):
-                back_copies[name, half].wait_recv()
+    def combine(half):
+        for name in ("high", "low", "far"):
+            back_copies[name, half].wait_recv()
 
         def body(n):
-            cols = columns(n, 256)
-            token_out[:, cols] = dot_rows(place[...], returned[:, cols]).astype(bf16)
-        loop(8, body)
+            cols = columns(n + 4 * half, 256)
+            token_out[:, cols] = dot(place_t[...], returned[:, cols]).astype(bf16)
+        loop(4, body)
 
     rows_a, rows_b = slice(0, ROWS_A), slice(ROWS_A, SHARE)
     copies = {}
@@ -447,22 +447,15 @@
             total = total + wide(bz_buf[slot])
         finish(total, rows_b)
 
-    def final_swap():
-        other = 1 - core
-        gate_rows = pl.ds(pl.multiple_of(32 * other, 32), 32)
-        last = [send(final.at[gate_rows], final_gate, bz_sem, (4,), partner)]
-        for k in range(2):
-            down_rows = pl.ds(pl.multiple_of(64 + 16 * k + 8 * other, 8), 8)
-            last.append(send(final.at[down_rows], final_down.at[k], bz_sem, (5 + k,), partner))
-        gate_out[:, my_units] = final[pl.ds(pl.multiple_of(32 * core, 32), 32)]
-        for k in range(2):
-            down_out[:, down_columns(k)] = final[pl.ds(pl.multiple_of(64 + 16 * k + 8 * core, 8), 8)]
-        for copy in last:
-            copy.wait_recv()
-        gate_out[:, their_units] = final_gate[...]
-        for k in range(2):
-            cols = pl.ds(pl.multiple_of(other * WIDTH + k * 512, 512), 512)
-            down_out[:, cols] = final_down[k]
+    def to_other_core(rows, index):
+        return send(final.at[rows], final_pair.at[rows], bz_sem, (4 + index,), partner)
+
+    def store_shares():
+        for source, units, first_col in ((final, my_units, core * WIDTH), (final_pair, their_units, (1 - core) * WIDTH)):
+            gate_out[:, units] = source[pl.ds(pl.multiple_of(32 * core, 32), 32)]
+            for k in range(2):
+                cols = pl.ds(pl.multiple_of(first_col + k * 512, 512), 512)
+                down_out[:, cols] = source[pl.ds(pl.multiple_of(64 + 16 * k + 8 * core, 8), 8)]
 
     upper = (4, 3, 2, 1)
     edge = {0: (2, 1), 1: (-1, 0)}
@@ -498,46 +491,51 @@
     for n in range(4):
         token_columns(n)
     give_back(0)
+    token_columns(4)
     a_step(2, True)
     b_start(-1)
-    token_columns(4)
+    token_columns(5)
+    token_columns(6)
     b_next(4)
     b_start(1)
     a_step(3, False)
+    token_columns(7)
+    give_back(1)
     b_next(-3)
-    token_columns(5)
     b_next(3)
     b_start(0)
-    token_columns(6)
     a_step(3, True)
     b_next(-2)
     b_y_end(4)
-    token_columns(7)
-    give_back(1)
     b_next(2)
-    b_y_end(-3)
     a_step(4, False)
-    b_y_end(3)
     b_next(-1)
     b_next(1)
+    b_y_end(-3)
+    b_y_end(3)
+    pass_on(0)
+    b_next(0)
+    a_step(4, True)
     b_y_end(-2)
-    a_step(4, True)
-    b_next(0)
     b_y_end(2)
-    pass_on(0)
     b_y_end(-1)
+    b_y_end(1)
+    pass_on(1)
     a_z_end(2)
     a_z_end(-1)
-    b_y_end(1)
     a_z_end(1)
     total_b = b_y_end(0)
     total_a = a_z_end(0)
-    pass_on(1)
     final[rows_a], final[rows_b] = total_a, total_b
-    combine()
+    combine(0)
+    b_end(final[rows_b])
+    last = [to_other_core(rows_b, 0)]
     a_end(final[rows_a])
-    b_end(final[rows_b])
-    final_swap()
+    last.append(to_other_core(rows_a, 1))
+    combine(1)
+    for copy in last:
+        copy.wait_recv()
+    store_shares()
     for copy in started:
         copy.wait_send()
 
@@ -561,7 +559,7 @@
         ((2, TOK), jnp.int32), ((2, TOK), f32),
         ((TOK, MODEL), bf16), ((TOK, MODEL), bf16), ((MODEL, WIDTH), bf16), ((UNITS, MODEL), bf16),
         ((UNITS, MODEL), bf16), ((WIDTH, MODEL), bf16), ((MODEL, UNITS), bf16),
-        ((ROWS, TOK), bf16), ((ROWS, TOK), f32), ((3 * CAP, MODEL), bf16), ((3 * CAP, MODEL), bf16),
+        ((ROWS, TOK), bf16), ((TOK, ROWS), bf16), ((ROWS, TOK), f32), ((3 * CAP, MODEL), bf16), ((3 * CAP, MODEL), bf16),
         ((CAP, MODEL), bf16), ((CAP, MODEL), bf16),
         ((ROWS, MODEL), bf16), ((ROWS, MODEL), bf16), ((ROWS, WIDTH), f32), ((ROWS, WIDTH), bf16),
         ((ROWS, UNITS), bf16), ((MODEL, HALF), f32), ((UNITS, WIDTH), f32),
@@ -571,7 +569,7 @@
         ((2 * CAP, UNITS), f32), ((CHIPS_Z, CHIPS_Y, SHARE, HALF), bf16),
         ((2, 4, CHIPS_Y, ROWS_A, HALF), bf16), ((3, ROWS_A, HALF), bf16),
         ((2, 2, CHIPS_Z, ROWS_B, HALF), bf16), ((2, 2, ROWS_B, HALF), bf16), ((4, ROWS_B, HALF), bf16),
-        ((SHARE, HALF), f32), ((GATE_ROWS, HALF), f32), ((2, DOWN_ROWS, HALF), f32),
+        ((SHARE, HALF), f32), ((SHARE, HALF), f32),
     )
     semaphores = ((7,), (2, 12), (2, 2, 4), (2, 12), (2, 2, 4, 4), (2, 3), (2, 2, 2, 8), (2, 2, 2), (2, 7))
     results = (

time: 77.2 us -> 74.5 us (0.965)
  Pallas kernels: 75.1 us -> 72.4 us
    pallas_call x1, Pallas kernels: 74.2 us -> 71.5 us  [on_device(): pl.pallas_call(layer_kernel, out_shape=results, in_specs=[pl.BlockSpec(me...]
where the time goes in v4:
time: 74.5 us; the launch traced here: 74.4 us
  Pallas kernels  72.4 us (97%)
  local copies, waits for them, and re-layouts  1.35 us (2%)
    pallas_call x1, Pallas kernels, on_device(): pl.pallas_call(layer_kernel, out_shape=results, in_specs=[pl.BlockSpec(me...  71.5 us

profile of v4, /device:TPU:1, one launch (start us, length us, event | category | flops | bytes accessed | tf_op | source)
XLA Modules:
  0.0 74.4 jit_solution(4769245981390416568)
XLA Ops:
  0.6 0.0 copy-start
  0.6 0.7 copy-done
  1.3 0.0 copy-start.1
  1.3 0.7 copy-done.1
  2.0 71.5 %shard_map.94 = (bf16[128,2048]{1,0:T(8,128)(2,1)S(1)}, f32[32,1024]{1,0:T(8,128)S(1)}, f32[8,2048]{1,0:T(8,128)S(1)}) custom-call(s32[2,128]{1,0:T(2,128)S(1)} %bitcast.7, f32[2,128]{1,0:T(2,128)S(1)} %bitcast.8, bf16[128,2048]{1,0:T(8,128)(2,1)} %tokens_hbm.1, bf16[128,2048]{1,0:T(8,128)(2,1)} %cotangent_hbm.1, bf16[2048,1024]{1,0:T(8,128)(2,1)} %bitcast.9, ...), custom_call_target="tpu_custom_call" | custom-call | tf_op jit(solution)/shard_map/pallas_call | solution.py:580
  73.5 0.9 %shard_map.95 = (bf16[128,2048]{1,0:T(8,128)(2,1)}, f32[32,1024]{1,0:T(8,128)}, f32[8,2048]{1,0:T(8,128)}) custom-call(bf16[128,2048]{1,0:T(8,128)(2,1)S(1)} %get-tuple-element.9.refs_0_, f32[32,1024]{1,0:T(8,128)S(1)} %get-tuple-element.10.refs_1_, f32[8,2048]{1,0:T(8,128)S(1)} %get-tuple-element.11.refs_2_), custom_call_target="tpu_custom_call" | custom-call | tf_op jit(solution)/shard_map/pallas_call | solution.py:592
Async XLA Ops:
  0.6 0.7 copy-start
  1.3 0.7 copy-start.1

commit v5 on v4

--- a/solution.py
+++ b/solution.py
@@ -293,10 +293,6 @@
         back[LATE, upper] = (value * both[LATE, upper]).astype(bf16)
     loop(2, late_pull)
     to_partner("back late", 11, back.at[LATE, their_units], back_pair.at[LATE])
-    def late_gate(n):
-        rows = columns(n, 256)
-        sum_gate[rows, :] += dot(tok_late[rows], back[LATE, my_units])
-    loop(8, late_gate)
     for name in ("grad low", "grad high", "hidden late"):
         pair[name].wait_recv()
 
@@ -313,7 +309,8 @@
     def group(off):
         zz = zi(off)
         rows = columns(zz, 256)
-        value = sum_gate[rows, :] + dot(tok_late_pair[rows], back_pair[LATE])
+        value = sum_gate[rows, :] + dot(tok_late[rows], back[LATE, my_units])
+        value = value + dot(tok_late_pair[rows], back_pair[LATE])
         for yy in range(CHIPS_Y):
             down_rows = pl.ds(pl.multiple_of(zz * 64 + yy * 16, 16), 16)
             own[zz, yy, 0:64] = value[64 * yy : 64 * yy + 64].astype(bf16)

time: 74.5 us -> 73 us (0.980)
  Pallas kernels: 72.4 us -> 70.9 us
    pallas_call x1, Pallas kernels: 71.5 us -> 70 us  [on_device(): pl.pallas_call(layer_kernel, out_shape=results, in_specs=[pl.BlockSpec(me...]
where the time goes in v5:
time: 73 us; the launch traced here: 72.9 us
  Pallas kernels  70.9 us (97%)
  local copies, waits for them, and re-layouts  1.35 us (2%)
    pallas_call x1, Pallas kernels, on_device(): pl.pallas_call(layer_kernel, out_shape=results, in_specs=[pl.BlockSpec(me...  70 us

profile of v5, /device:TPU:1, one launch (start us, length us, event | category | flops | bytes accessed | tf_op | source)
XLA Modules:
  0.0 72.9 jit_solution(6255563314383273789)
XLA Ops:
  0.6 0.0 copy-start
  0.6 0.7 copy-done
  1.3 0.0 copy-start.1
  1.3 0.7 copy-done.1
  2.0 70.0 %shard_map.94 = (bf16[128,2048]{1,0:T(8,128)(2,1)S(1)}, f32[32,1024]{1,0:T(8,128)S(1)}, f32[8,2048]{1,0:T(8,128)S(1)}) custom-call(s32[2,128]{1,0:T(2,128)S(1)} %bitcast.7, f32[2,128]{1,0:T(2,128)S(1)} %bitcast.8, bf16[128,2048]{1,0:T(8,128)(2,1)} %tokens_hbm.1, bf16[128,2048]{1,0:T(8,128)(2,1)} %cotangent_hbm.1, bf16[2048,1024]{1,0:T(8,128)(2,1)} %bitcast.9, ...), custom_call_target="tpu_custom_call" | custom-call | tf_op jit(solution)/shard_map/pallas_call | solution.py:577
  72.0 0.9 %shard_map.95 = (bf16[128,2048]{1,0:T(8,128)(2,1)}, f32[32,1024]{1,0:T(8,128)}, f32[8,2048]{1,0:T(8,128)}) custom-call(bf16[128,2048]{1,0:T(8,128)(2,1)S(1)} %get-tuple-element.9.refs_0_, f32[32,1024]{1,0:T(8,128)S(1)} %get-tuple-element.10.refs_1_, f32[8,2048]{1,0:T(8,128)S(1)} %get-tuple-element.11.refs_2_), custom_call_target="tpu_custom_call" | custom-call | tf_op jit(solution)/shard_map/pallas_call | solution.py:589
Async XLA Ops:
  0.6 0.7 copy-start
  1.3 0.7 copy-start.1

commit v6 on v5

--- a/solution.py
+++ b/solution.py
@@ -268,12 +268,6 @@
     for name in ("tok early", "back early"):
         pair[name].wait_recv()
 
-    def early_gate(n):
-        rows = columns(n, 256)
-        value = dot(tok_early[rows], back[EARLY, my_units])
-        sum_gate[rows, :] = value + dot(tok_early_pair[rows], back_pair[EARLY])
-    loop(8, early_gate)
-
     swap["grad", 0, 0].wait_recv()
     to_partner("grad low", 9, grad_all.at[LOW, theirs], grad_pair.at[LOW])
     swap["grad", 1, 0].wait_recv()
@@ -309,7 +303,9 @@
     def group(off):
         zz = zi(off)
         rows = columns(zz, 256)
-        value = sum_gate[rows, :] + dot(tok_late[rows], back[LATE, my_units])
+        value = dot(tok_early[rows], back[EARLY, my_units])
+        value = value + dot(tok_early_pair[rows], back_pair[EARLY])
+        value = value + dot(tok_late[rows], back[LATE, my_units])
         value = value + dot(tok_late_pair[rows], back_pair[LATE])
         for yy in range(CHIPS_Y):
             down_rows = pl.ds(pl.multiple_of(zz * 64 + yy * 16, 16), 16)

time: 73 us -> 72.4 us (level)
  no operation moved by 1% of the time
where the time goes in v6:
time: 72.4 us; the launch traced here: 72.3 us
  Pallas kernels  70.3 us (97%)
  local copies, waits for them, and re-layouts  1.35 us (2%)
    pallas_call x1, Pallas kernels, on_device(): pl.pallas_call(layer_kernel, out_shape=results, in_specs=[pl.BlockSpec(me...  69.4 us

profile of v6, /device:TPU:1, one launch (start us, length us, event | category | flops | bytes accessed | tf_op | source)
XLA Modules:
  0.0 72.3 jit_solution(15184444025777083915)
XLA Ops:
  0.6 0.0 copy-start
  0.6 0.7 copy-done
  1.3 0.0 copy-start.1
  1.3 0.7 copy-done.1
  2.0 69.4 %shard_map.94 = (bf16[128,2048]{1,0:T(8,128)(2,1)S(1)}, f32[32,1024]{1,0:T(8,128)S(1)}, f32[8,2048]{1,0:T(8,128)S(1)}) custom-call(s32[2,128]{1,0:T(2,128)S(1)} %bitcast.7, f32[2,128]{1,0:T(2,128)S(1)} %bitcast.8, bf16[128,2048]{1,0:T(8,128)(2,1)} %tokens_hbm.1, bf16[128,2048]{1,0:T(8,128)(2,1)} %cotangent_hbm.1, bf16[2048,1024]{1,0:T(8,128)(2,1)} %bitcast.9, ...), custom_call_target="tpu_custom_call" | custom-call | tf_op jit(solution)/shard_map/pallas_call | solution.py:573
  71.4 0.9 %shard_map.95 = (bf16[128,2048]{1,0:T(8,128)(2,1)}, f32[32,1024]{1,0:T(8,128)}, f32[8,2048]{1,0:T(8,128)}) custom-call(bf16[128,2048]{1,0:T(8,128)(2,1)S(1)} %get-tuple-element.9.refs_0_, f32[32,1024]{1,0:T(8,128)S(1)} %get-tuple-element.10.refs_1_, f32[8,2048]{1,0:T(8,128)S(1)} %get-tuple-element.11.refs_2_), custom_call_target="tpu_custom_call" | custom-call | tf_op jit(solution)/shard_map/pallas_call | solution.py:585
Async XLA Ops:
  0.6 0.7 copy-start
  1.3 0.7 copy-start.1
